TPU v7x, 512 devices: a whole 4x4x16 slice. The times are simulated.
512 devices in a mesh: rows: 32 (over z, core), mem: 16 (over y, x).
Axes of the slice: x: 4, y: 4, z: 16, core: 2. Of those that a mesh axis runs over, the one named last changes fastest.
Arguments:
- ensemble_state: float32 [16384, 4096], P('rows', 'mem'), may hold values from -6 to 6
- predicted: float32 [12288, 4096], P('rows', 'mem'), may hold values from -6 to 6
- perturbed: float32 [12288, 4096], P('rows', 'mem'), may hold values from -9 to 9
- obs_variance: float32 [3, 256], replicated, may hold values from 0.25 to 4
- owners: int32 [3], replicated, may hold values from 0 to 31, as said below
- positions: int32 [3, 256], replicated, may hold values from 0 to 383, as said below
Outputs:
- analysis_state: float32 [16384, 4096], P('rows', 'mem')
- analysis_obs: float32 [12288, 4096], P('rows', 'mem')
Inputs may be any that keep to these rules, and one draw needn't show every extreme that they name: The 3 owners are distinct; the first and the last index of rows are always among them. Each batch's 256 positions are distinct; every batch holds position 0 and position 383.
All inputs are finite; a program needn't handle non-finite values.
Results may differ from a plain program's by a relative error of at most 0.0003.
Values sent between devices are 32-bit elements; how exact they have to be, the bound alone decides.
No kernel may reach another device: no remote copies, remote signals or barrier semaphores. Data moves between devices by JAX's collectives and lax.ppermute only.
A program may use at most 64 MiB of HBM per device.

v0:
```python
import functools

import jax
import jax.numpy as jnp
from jax import lax
from jax.experimental import pallas as pl
from jax.experimental.pallas import tpu as pltpu
from jax.sharding import PartitionSpec as P

exact = lax.Precision.HIGHEST
HALF_A = ((0, 0), (1, 0), (2, 0), (1, 1), (2, 1), (2, 2))
HALF_B = ((1, 3), (2, 3), (3, 3), (2, 4), (3, 4), (4, 4))


def mm(a, b):
    return lax.dot_general(a, b, (((1,), (0,)), ((), ())), precision=exact, preferred_element_type=jnp.float32)


def mm_nt(a, b):
    return lax.dot_general(a, b, (((1,), (1,)), ((), ())), precision=exact, preferred_element_type=jnp.float32)


def mm_tn(a, b):
    return lax.dot_general(a, b, (((0,), (0,)), ((), ())), precision=exact, preferred_element_type=jnp.float32)


TILE = 8
LANES = 128


def split3(x):
    hi = x.astype(jnp.bfloat16)
    rest = x - hi.astype(jnp.float32)
    mid = rest.astype(jnp.bfloat16)
    low = (rest - mid.astype(jnp.float32)).astype(jnp.bfloat16)
    return hi, mid, low


def tn_narrow(a, b):
    ah, am, al = split3(a)
    bh, bm, bl = split3(b)
    left = jnp.concatenate([ah, ah, am, ah, am, al], axis=0)
    right = jnp.concatenate([bh, bm, bh, bl, bm, bh], axis=0)
    return lax.dot_general(left, right, (((0,), (0,)), ((), ())), preferred_element_type=jnp.float32)


def sweep_tiles(w, width):
    lane = lax.broadcasted_iota(jnp.int32, (TILE, LANES), 1)
    sub = lax.broadcasted_iota(jnp.int32, (TILE, LANES), 0)
    full = (TILE, LANES)
    n = width // TILE
    for s in range(n):
        off = s * TILE
        own = (lane >= off) & (lane < off + TILE)
        eye = jnp.where(lane - off == sub, 1.0, 0.0).astype(jnp.float32)
        cols = [[jnp.broadcast_to(w[t][0][:, off + j : off + j + 1], full) for j in range(TILE)] for t in range(n)]
        c = {}
        for j in range(TILE):
            for i in range(j, TILE):
                c[i, j] = jnp.broadcast_to(cols[s][j][i : i + 1, :], full)
        get = lambda i, j: c[max(i, j), min(i, j)]
        for j in range(TILE):
            r = 1.0 / c[j, j]
            old = {i: get(i, j) for i in range(TILE) if i != j}
            scaled = {i: old[i] * r for i in old}
            for k in range(TILE):
                for i in range(k, TILE):
                    if i != j and k != j:
                        c[i, k] = c[i, k] - scaled[i] * old[k]
            for i in old:
                c[max(i, j), min(i, j)] = scaled[i]
            c[j, j] = -r
        tcol = []
        for j in range(TILE):
            col = get(0, j)
            for i in range(1, TILE):
                col = jnp.where(sub == i, get(i, j), col)
            tcol.append(-col)
        rows, alt = [], []
        for h in range(len(w[0])):
            bz = jnp.where(own, eye, w[s][h]) if h == 0 else w[s][h]
            acc = tcol[0] * jnp.broadcast_to(bz[0:1, :], full)
            for j in range(1, TILE):
                acc = acc + tcol[j] * jnp.broadcast_to(bz[j : j + 1, :], full)
            rows.append(jnp.where(own, -acc, acc) if h == 0 else acc)
            alt.append(jnp.where(own, eye - acc, acc) if h == 0 else acc)
        spread = [[jnp.broadcast_to(a[j : j + 1, :], full) for j in range(TILE)] for a in alt]
        for t in range(n):
            if t == s:
                w[t] = rows
                continue
            new = []
            for h in range(len(alt)):
                acc = cols[t][0] * spread[h][0]
                for j in range(1, TILE):
                    acc = acc + cols[t][j] * spread[h][j]
                new.append(w[t][h] - acc)
            w[t] = new
    return w


def invert_in_place(a_ref, width=32):
    n = a_ref.shape[0]
    lane = lax.broadcasted_iota(jnp.int32, (width, n), 1)
    sub = lax.broadcasted_iota(jnp.int32, (width, n), 0)

    def step(b, _):
        base = pl.multiple_of(b * width, width)
        panel = a_ref[pl.ds(base, width), :]
        rolled = pltpu.roll(panel, lax.rem(n - base, n), 1)
        w = [
            [rolled[t * TILE : (t + 1) * TILE, h * LANES : (h + 1) * LANES] for h in range(n // LANES)]
            for t in range(width // TILE)
        ]
        w = sweep_tiles(w, width)
        w = jnp.concatenate([jnp.concatenate(row, axis=1) for row in w], axis=0)
        w = pltpu.roll(w, base, 1)
        inside = (lane >= base) & (lane < base + width)
        eye = jnp.where(lane - base == sub, 1.0, 0.0).astype(jnp.float32)
        a_ref[...] = a_ref[...] - tn_narrow(panel, jnp.where(inside, eye + w, w))
        a_ref[pl.ds(base, width), :] = w
        return 0

    lax.fori_loop(0, n // width, step, 0)
    a_ref[...] = -a_ref[...]


def chain_kernel(local, scale, core_ref, here_ref, there_ref, dev_ref, r_ref, e_ref, v_ref, inv0, inv1, inv2, k_ref, t_ref, g_ref):
    p = r_ref.shape[1]
    first = core_ref[0] == 0
    eye = lax.broadcasted_iota(jnp.int32, (p, p), 0) == lax.broadcasted_iota(jnp.int32, (p, p), 1)

    def block(i, j):
        half, n = (0, HALF_A.index((i, j))) if (i, j) in HALF_A else (1, HALF_B.index((i, j)))
        mine, other = here_ref[n * p : (n + 1) * p, :], there_ref[n * p : (n + 1) * p, :]
        total = jnp.where(first, mine, other) if half == 0 else jnp.where(first, other, mine)
        between = tn_narrow(dev_ref[:, i * p : (i + 1) * p], dev_ref[:, j * p : (j + 1) * p])
        return (total + local * between) * scale

    def add_diag(x, n):
        return x + jnp.where(eye, r_ref[n : n + 1, :], 0.0)

    inv0[...] = add_diag(block(0, 0), 0)
    invert_in_place(inv0)
    k_ref[0:p, :] = mm(block(1, 0), inv0[...])
    k_ref[p : 2 * p, :] = mm(block(2, 0), inv0[...])
    g_ref[0] = block(3, 3)
    g_ref[1] = block(1, 3)
    g_ref[2] = block(2, 3)
    g_ref[3] = block(3, 4)
    kh = mm(k_ref[...], 0.5 * g_ref[0])
    t_ref[0:p, :] = g_ref[1] + kh[:p]
    t_ref[p : 2 * p, :] = g_ref[2] + kh[p:]
    t_ref[2 * p :, :] = g_ref[3].T - kh[:p]
    z1 = mm_nt(k_ref[0:p, :], t_ref[...])
    z2 = mm_nt(k_ref[p : 2 * p, :], t_ref[...])
    inv1[...] = add_diag(block(1, 1) + z1[:, :p] + z1[:, :p].T, 1)
    c21 = block(2, 1) + z2[:, :p] + z1[:, p : 2 * p].T
    c22 = block(2, 2) + z2[:, p : 2 * p] + z2[:, p : 2 * p].T
    ce2 = block(2, 4).T - z1[:, p : 2 * p] + z2[:, 2 * p :].T
    cee = block(4, 4) - z1[:, 2 * p :] - z1[:, 2 * p :].T
    t_ref[0:p, :] = ce2
    t_ref[p : 2 * p, :] = cee
    invert_in_place(inv1)
    k21 = mm(c21, inv1[...])
    kh = mm(k21, t_ref[p : 2 * p, :])
    z = mm_nt(k21, t_ref[0:p, :].T + 0.5 * kh)
    inv2[...] = add_diag(c22 + z + z.T, 2)
    invert_in_place(inv2)
    e0 = e_ref[0:p, :]
    ke = mm(k_ref[...], e0)
    e1 = e_ref[p : 2 * p, :] - ke[:p]
    e2 = e_ref[2 * p :, :] - ke[p:] - mm(k21, e1)
    w2 = mm(inv2[...], e2)
    v_ref[2 * p : 3 * p, :] = w2 * scale
    w1 = mm(inv1[...], e1 + mm(t_ref[0:p, :] + kh.T, w2))
    v_ref[p : 2 * p, :] = w1 * scale
    k21w2 = mm_tn(k21, w2)
    v_ref[4 * p :, :] = k21w2 * scale
    v3 = mm_tn(k_ref[0:p, :], w1 - k21w2) + mm_tn(k_ref[p : 2 * p, :], w2)
    v_ref[3 * p : 4 * p, :] = v3 * scale
    w0 = e0 + mm_tn(g_ref[1], w1) + mm_tn(g_ref[2], w2) + mm(g_ref[0], v3) + mm(g_ref[3], k21w2)
    v_ref[0:p, :] = mm(inv0[...], w0) * scale


def chain(core, here, there, dev, r, e, local, scale):
    p = r.shape[1]
    vm = pl.BlockSpec(memory_space=pltpu.VMEM)
    return pl.pallas_call(
        functools.partial(chain_kernel, local, scale),
        out_shape=jax.ShapeDtypeStruct((5 * p, e.shape[1]), jnp.float32),
        in_specs=[pl.BlockSpec(memory_space=pltpu.SMEM)] + [vm] * 5,
        out_specs=vm,
        scratch_shapes=[pltpu.VMEM((p, p), jnp.float32)] * 3
        + [pltpu.VMEM((2 * p, p), jnp.float32), pltpu.VMEM((3 * p, p), jnp.float32), pltpu.VMEM((4, p, p), jnp.float32)],
        name="chain",
    )(core, here, there, dev, r, e)


def prepare_kernel(core_ref, here_ref, there_ref, state_ref, pred_ref, inno_ref, cross_x_ref, cross_h_ref, pay_ref, y_ref):
    p, local = inno_ref.shape[0] // 3, inno_ref.shape[1]
    n_mem, part = pay_ref.shape[0], here_ref.shape[2] // 2
    first = core_ref[0] == 0
    for b in range(3):
        mine, other = here_ref[:, b], there_ref[:, b]
        even = jnp.where(first, mine, other)
        odd = jnp.where(first, other, mine)
        obs = jnp.concatenate([even[:, :part], odd[:, :part]], axis=1).reshape(p, local)
        pert = jnp.concatenate([even[:, part:], odd[:, part:]], axis=1).reshape(p, local)
        inno = pert - obs
        inno_ref[b * p : (b + 1) * p, :] = inno
        y_ref[b * p : (b + 1) * p, :] = obs
        if b < 2:
            y_ref[(3 + b) * p : (4 + b) * p, :] = inno
    ones = jnp.ones((TILE, local), jnp.float32)
    n_gram = 6 * p // n_mem
    row = n_gram

    def extra(values):
        nonlocal row
        for at in range(0, values.shape[1], p):
            piece = values[0:1, at : at + p]
            if piece.shape[1] < p:
                piece = jnp.concatenate([piece, jnp.zeros((1, p - piece.shape[1]), jnp.float32)], axis=1)
            pay_ref[:, row : row + 1, :] = jnp.broadcast_to(piece[None], (n_mem, 1, p))
            row += 1

    pay_ref[:, n_gram:, :] = jnp.zeros((n_mem, pay_ref.shape[1] - n_gram, p), jnp.float32)
    extra(mm_nt(ones, y_ref[...]) * (1.0 / local))
    extra(jnp.concatenate([mm_nt(ones, state_ref[...]), mm_nt(ones, pred_ref[...])], axis=1))
    for i in range(5):
        rows = y_ref[i * p : (i + 1) * p, :]
        y_ref[i * p : (i + 1) * p, :] = rows - jnp.sum(rows, axis=1, keepdims=True) * (1.0 / local)

    def products(pairs):
        for n, (i, j) in enumerate(pairs):
            block = mm_nt(y_ref[i * p : (i + 1) * p, :], y_ref[j * p : (j + 1) * p, :])
            at = 0
            while at < p:
                dest, off = divmod(n * p + at, n_gram)
                size = min(n_gram - off, p - at)
                pay_ref[dest, off : off + size, :] = block[at : at + size]
                at += size

    @pl.when(first)
    def _():
        products(HALF_A)

    @pl.when(jnp.logical_not(first))
    def _():
        products(HALF_B)

    for src_ref, out_ref in ((state_ref, cross_x_ref), (pred_ref, cross_h_ref)):
        chunk = 128

        def step(n, _, src_ref=src_ref, out_ref=out_ref):
            at = pl.ds(pl.multiple_of(n * chunk, chunk), chunk)
            out_ref[at, :] = mm_nt(src_ref[at, :], y_ref[...])
            return 0

        lax.fori_loop(0, src_ref.shape[0] // chunk, step, 0)


def prepare(core, here, there, state, predicted, n_mem):
    p, local = here.shape[0] * here.shape[2], state.shape[1]
    n_gram = 6 * p // n_mem
    n_extra = 5 + -(-(state.shape[0] + predicted.shape[0]) // p)
    vm = pl.BlockSpec(memory_space=pltpu.VMEM)
    return pl.pallas_call(
        prepare_kernel,
        out_shape=[
            jax.ShapeDtypeStruct((3 * p, local), jnp.float32),
            jax.ShapeDtypeStruct((state.shape[0], 5 * p), jnp.float32),
            jax.ShapeDtypeStruct((predicted.shape[0], 5 * p), jnp.float32),
            jax.ShapeDtypeStruct((n_mem, n_gram + -(-n_extra // TILE) * TILE, p), jnp.float32),
        ],
        in_specs=[pl.BlockSpec(memory_space=pltpu.SMEM)] + [vm] * 4,
        out_specs=[vm] * 4,
        scratch_shapes=[pltpu.VMEM((5 * p, local), jnp.float32)],
        name="prepare",
    )(core, here, there, state, predicted)


def make(n_rows, n_mem):
    cores = 2
    n_z = n_rows // cores
    same_core = [[z * cores + c for z in range(n_z)] for c in range(cores)]
    swap = [(i, i ^ 1) for i in range(n_rows)]

    def on_device(state, predicted, perturbed, obs_variance, owners, positions):
        p = positions.shape[1]
        local = state.shape[1]
        members = local * n_mem
        part = p // n_rows
        row = lax.axis_index("rows")
        core = row % cores

        mine = jnp.argmax(owners == row)
        picked = positions[mine]
        out = jnp.concatenate(
            [
                jnp.take(predicted, picked, axis=0).reshape(n_rows, part, local),
                jnp.take(perturbed, picked, axis=0).reshape(n_rows, part, local),
            ],
            axis=1,
        )
        got = lax.all_to_all(out, "rows", 0, 0, tiled=True)
        piece = jnp.take(got, owners, axis=0)
        here = lax.all_gather(piece, "rows", axis_index_groups=same_core)
        there = lax.ppermute(here, "rows", swap)
        which = core.reshape(1).astype(jnp.int32)
        inno, cross_x, cross_h, payload = prepare(which, here, there, state, predicted, n_mem)
        n_gram = 6 * p // n_mem
        n_state = state.shape[0] + predicted.shape[0]
        cross_x, cross_h = lax.psum((cross_x, cross_h), "mem")
        got = lax.all_to_all(payload, "mem", 0, 0, tiled=True)
        summed = jnp.sum(got[:, :n_gram], axis=0)
        extra = got[:, n_gram:].reshape(n_mem, -1)
        mu_all = extra[:, : 5 * p]
        sums_all = extra[:, 5 * p : 5 * p + n_state]
        here = lax.all_to_all(
            jnp.broadcast_to(summed[None], (n_mem, n_gram, p)), "mem", 0, 0, tiled=True
        ).reshape(6 * p, p)
        there = lax.ppermute(here, "rows", swap)
        dev = mu_all - jnp.sum(mu_all, axis=0, keepdims=True) / n_mem
        v = chain(
            which,
            here,
            there,
            dev,
            obs_variance,
            inno,
            float(local),
            1.0 / (members - 1),
        )
        between = mm(dev, v)
        n_x = state.shape[0]
        new_state = state + mm(cross_x, v) + mm_tn(sums_all[:, :n_x], between)
        new_obs = predicted + mm(cross_h, v) + mm_tn(sums_all[:, n_x:], between)
        return new_state, new_obs

    return on_device


def solution(mesh):
    in_specs = (P("rows", "mem"), P("rows", "mem"), P("rows", "mem"), P(), P(), P())
    out_specs = (P("rows", "mem"), P("rows", "mem"))
    inner = make(mesh.shape["rows"], mesh.shape["mem"])

    return jax.shard_map(
        inner,
        mesh=mesh,
        in_specs=in_specs,
        out_specs=out_specs,
        check_vma=False,
    )
```

profile of v0, /device:TPU:6, one launch (start us, length us, event | category | flops | bytes accessed | tf_op | source)
XLA Modules:
  0.0 291.8 jit_solution(1401336195135285898)
XLA Ops:
  7.2 1.4 compare_reduce_fusion
  10.5 0.7 constant_dynamic-slice_fusion
  11.2 2.0 gather_fusion.1
  13.2 1.0 gather_fusion.2
  14.2 0.1 select_bitcast_fusion.1
  14.3 0.8 pad_maximum_fusion
  15.1 15.5 %all-to-all-start = ((f32[32,16,256]{2,1,0:T(8,128)}), f32[32,16,256]{2,1,0:T(8,128)S(1)}, u32[]{:S(2)}, u32[]{:S(2)}) async-start(f32[32,16,256]{2,1,0:T(8,128)} %pad_maximum_fusion), calls=%async_computation | async-start | bytes 1048576 | tf_op jit(solution)/shard_map/all_to_all | solution.py:307
  30.6 33.7 %all-to-all-done = f32[32,16,256]{2,1,0:T(8,128)S(1)} async-done(((f32[32,16,256]{2,1,0:T(8,128)}), f32[32,16,256]{2,1,0:T(8,128)S(1)}, u32[]{:S(2)}, u32[]{:S(2)}) %all-to-all-start) | async-done | bytes 524320 | tf_op jit(solution)/shard_map/all_to_all | solution.py:307
  64.4 0.6 gather_fusion
  65.0 30.6 %all_gather.4.here_ref = f32[16,3,16,256]{3,2,1,0:T(8,128)S(1)} all-gather(f32[1,3,16,256]{3,2,1,0:T(8,128)S(1)} %bitcast_select_fusion), channel_id=1, replica_groups={{0,32,64,96,128,160,192,224,256,288,320,352,384,416,448,480},{16,48,80,..., dimensions={0}, use_global_device_ids=true | all-gather | bytes 835584 | tf_op jit(solution)/shard_map/all_gather | solution.py:309
  95.6 1.9 collective-permute-start
  97.6 2.2 collective-permute-done.there_ref
  99.8 1.0 copy-done.8
  100.8 16.5 %prepare.1 = (f32[768,256]{1,0:T(8,128)}, f32[512,1280]{1,0:T(8,128)}, f32[384,1280]{1,0:T(8,128)}, f32[16,112,256]{2,1,0:T(8,128)}) custom-call(s32[1]{0:T(128)} %bitcast.core_ref, f32[16,3,16,256]{3,2,1,0:T(8,128)} %copy-done.4, f32[16,3,16,256]{3,2,1,0:T(8,128)} %copy-done.8, f32[512,256]{1,0:T(8,128)} %state_ref.1, f32[384,256]{1,0:T(8,128)} %pred_ref.1), custom_call_target="tpu_custom_call" | custom-call | tf_op jit(solution)/shard_map/prepare/pallas_call | solution.py:269
  117.3 7.4 %all-to-all-start.1 = ((f32[16,112,256]{2,1,0:T(8,128)}), f32[16,112,256]{2,1,0:T(8,128)S(1)}, u32[]{:S(2)}, u32[]{:S(2)}) async-start(f32[16,112,256]{2,1,0:T(8,128)} %get-tuple-element.10), calls=%async_computation.1 | async-start | bytes 3670016 | tf_op jit(solution)/shard_map/all_to_all | solution.py:316
  124.7 0.7 all-reduce.3.cloned.1.call-update
  125.4 31.7 %all-to-all-done.1 = f32[16,112,256]{2,1,0:T(8,128)S(1)} async-done(((f32[16,112,256]{2,1,0:T(8,128)}), f32[16,112,256]{2,1,0:T(8,128)S(1)}, u32[]{:S(2)}, u32[]{:S(2)}) %all-to-all-start.1) | async-done | bytes 1835040 | tf_op jit(solution)/shard_map/all_to_all | solution.py:316
  157.1 0.1 slice_reduce_fusion
  157.2 0.1 broadcast_in_dim.31
  157.3 27.5 %all_to_all.15 = f32[16,96,256]{2,1,0:T(8,128)S(1)} all-to-all(f32[16,96,256]{2,1,0:T(8,128)S(1)} %broadcast_in_dim.31), channel_id=1, replica_groups=mesh['rows'=32,'mem'=16] {'mem'}, dimensions={0} | all-to-all | bytes 3145728 | tf_op jit(solution)/shard_map/all_to_all | solution.py:321
  184.8 2.1 collective-permute-start.1
  186.9 0.2 copy.8
  187.1 0.6 slice_subtract_fusion.dev_ref
  187.8 2.3 collective-permute-done.1.there_ref
  190.1 1.1 copy-done.7
  191.2 49.4 %chain.1 = f32[1280,256]{1,0:T(8,128)} custom-call(s32[1]{0:T(128)} %bitcast.core_ref, f32[1536,256]{1,0:T(8,128)} %bitcast.20, f32[1536,256]{1,0:T(8,128)} %copy-done.7, f32[16,1280]{1,0:T(8,128)} %slice_subtract_fusion.dev_ref, f32[3,256]{1,0:T(4,128)} %r_ref.1, f32[768,256]{1,0:T(8,128)} %get-tuple-element.11.e_ref), custom_call_target="tpu_custom_call" | custom-call | tf_op jit(solution)/shard_map/chain/pallas_call | solution.py:189
  240.6 2.1 fusion.6
  242.7 0.5 fusion.4
  243.2 0.6 fusion.2
  243.9 33.9 %all-reduce.3.cloned.1.call-done = (f32[512,1280]{1,0:T(8,128)}, f32[384,1280]{1,0:T(8,128)}) async-done(((f32[512,1280]{1,0:T(8,128)}, f32[384,1280]{1,0:T(8,128)}), (f32[512,1280]{1,0:T(8,128)}, f32[384,1280]{1,0:T(8,128)})) %all-reduce.3.cloned.1.call-update) | async-done | bytes 4587536 | tf_op jit(solution)/shard_map/psum | solution.py:315
  277.8 4.2 %fusion.1 = f32[384,256]{1,0:T(8,128)} fusion(f32[384,256]{1,0:T(8,128)S(1)} %fusion.4, f32[384,256]{1,0:T(8,128)S(1)} %copy-done.1, f32[384,1280]{1,0:T(8,128)} %get-tuple-element.14, f32[1280,256]{1,0:T(8,128)S(1)} %copy-done.2), kind=kOutput, calls=%fused_computation.7 | convolution fusion | flops 1510146048 | bytes 4456448 | tf_op jit(solution)/shard_map/dot_general | solution.py:16
  281.9 3.1 %fusion = f32[512,256]{1,0:T(8,128)} fusion(f32[512,256]{1,0:T(8,128)S(1)} %fusion.2, f32[512,256]{1,0:T(8,128)S(1)} %copy-done.6, f32[512,1280]{1,0:T(8,128)S(1)} %copy-done.5, f32[1280,256]{1,0:T(8,128)S(1)} %copy-done.2), kind=kOutput, calls=%fused_computation.5 | convolution fusion | flops 2013528064 | bytes 5505024 | tf_op jit(solution)/shard_map/dot_general | solution.py:16
  (31 shorter events, 0.2 us)
Async XLA Ops:
  7.2 6.0 %copy-start = (f32[384,256]{1,0:T(8,128)S(1)}, f32[384,256]{1,0:T(8,128)}, u32[]{:S(2)}) copy-start(f32[384,256]{1,0:T(8,128)} %param.10) | copy-start | bytes 1179652
  14.2 16.4 %copy-start.10 = (s32[3]{0:T(128)S(1)}, s32[3]{0:T(128)}, u32[]{:S(2)}) copy-start(s32[3]{0:T(128)} %param.12) | copy-start | bytes 40
  15.1 49.3 %all-to-all-start = ((f32[32,16,256]{2,1,0:T(8,128)}), f32[32,16,256]{2,1,0:T(8,128)S(1)}, u32[]{:S(2)}, u32[]{:S(2)}) async-start(f32[32,16,256]{2,1,0:T(8,128)} %pad_maximum_fusion), calls=%async_computation | async-start | bytes 1048576 | tf_op jit(solution)/shard_map/all_to_all | solution.py:307
  95.6 4.2 %copy-start.4 = (f32[16,3,16,256]{3,2,1,0:T(8,128)}, f32[16,3,16,256]{3,2,1,0:T(8,128)S(1)}, u32[]{:S(2)}) copy-start(f32[16,3,16,256]{3,2,1,0:T(8,128)S(1)} %all_gather.4.here_ref) | copy-start | bytes 2359300
  95.6 4.2 %collective-permute-start = (f32[16,3,16,256]{3,2,1,0:T(8,128)S(1)}, f32[16,3,16,256]{3,2,1,0:T(8,128)S(1)}, u32[]{:S(2)}, u32[]{:S(2)}) collective-permute-start(f32[16,3,16,256]{3,2,1,0:T(8,128)S(1)} %all_gather.4.here_ref), channel_id=1, source_target_pairs={{0,16},{16,0},{32,48},{48,32},{64,80},{80,64},{96,112},{112,96},{1... | collective-permute-start | bytes 2359304 | tf_op jit(solution)/shard_map/ppermute | solution.py:310
  99.8 1.0 copy-start.8
  117.3 39.8 %all-to-all-start.1 = ((f32[16,112,256]{2,1,0:T(8,128)}), f32[16,112,256]{2,1,0:T(8,128)S(1)}, u32[]{:S(2)}, u32[]{:S(2)}) async-start(f32[16,112,256]{2,1,0:T(8,128)} %get-tuple-element.10), calls=%async_computation.1 | async-start | bytes 3670016 | tf_op jit(solution)/shard_map/all_to_all | solution.py:316
  124.7 153.1 %all-reduce.3.cloned.1.call-start = ((), (), s32[]{:S(2)}) async-start(), calls=%async_computation.3 | async-start | bytes 9175040 | tf_op jit(solution)/shard_map/psum | solution.py:315
  184.8 2.1 copy-start.3
  184.8 5.3 %collective-permute-start.1 = (f32[1536,256]{1,0:T(8,128)S(1)}, f32[1536,256]{1,0:T(8,128)S(1)}, u32[]{:S(2)}, u32[]{:S(2)}) collective-permute-start(f32[1536,256]{1,0:T(8,128)S(1)} %bitcast.19), channel_id=1, source_target_pairs={{0,16},{16,0},{32,48},{48,32},{64,80},{80,64},{96,112},{112,96},{1... | collective-permute-start | bytes 4718600 | tf_op jit(solution)/shard_map/ppermute | solution.py:324
  190.1 1.1 copy-start.7
  191.2 49.4 %copy-start.9 = (f32[16,1280]{1,0:T(8,128)S(1)}, f32[16,1280]{1,0:T(8,128)}, u32[]{:S(2)}) copy-start(f32[16,1280]{1,0:T(8,128)} %slice_subtract_fusion.dev_ref) | copy-start | bytes 245764
  240.6 37.1 %copy-start.1 = (f32[384,256]{1,0:T(8,128)S(1)}, f32[384,256]{1,0:T(8,128)}, u32[]{:S(2)}) copy-start(f32[384,256]{1,0:T(8,128)} %pred_ref.1) | copy-start | bytes 1179652
  240.6 37.1 %copy-start.2 = (f32[1280,256]{1,0:T(8,128)S(1)}, f32[1280,256]{1,0:T(8,128)}, u32[]{:S(2)}) copy-start(f32[1280,256]{1,0:T(8,128)} %chain.1) | copy-start | bytes 3932164
  277.8 4.2 %copy-start.5 = (f32[512,1280]{1,0:T(8,128)S(1)}, f32[512,1280]{1,0:T(8,128)}, u32[]{:S(2)}) copy-start(f32[512,1280]{1,0:T(8,128)} %get-tuple-element.13) | copy-start | bytes 7864324
  277.8 4.2 %copy-start.6 = (f32[512,256]{1,0:T(8,128)S(1)}, f32[512,256]{1,0:T(8,128)}, u32[]{:S(2)}) copy-start(f32[512,256]{1,0:T(8,128)} %state_ref.1) | copy-start | bytes 1572868
Sparse Core Ops, SparseCore 0:
  129.0 148.7 all-reduce.2
where the time goes:
time: 293 us; the launch traced here: 292 us
  waiting for transfers between devices  105 us (36%)
  Pallas kernels  65.9 us (22%)
  blocking collectives  58.1 us (20%)
  starting transfers between devices  26.9 us (9%)
  between operations  16.2 us (6%)
  matrix products  10.4 us (4%)
  local copies, waits for them, and re-layouts  6.64 us (2%)
  other arithmetic  3.17 us (1%)
    pallas_call x1, Pallas kernels, chain(): pl.pallas_call(functools.partial(chain_kernel, local, scale), out_shape=j...  49.4 us
    psum x1, waiting for transfers between devices, on_device(): cross_x, cross_h = lax.psum((cross_x, cross_h), 'mem')  33.9 us
    all_to_all x1, waiting for transfers between devices, on_device(): got = lax.all_to_all(out, 'rows', 0, 0, tiled=True)  33.7 us
    all_to_all x1, waiting for transfers between devices, on_device(): got = lax.all_to_all(payload, 'mem', 0, 0, tiled=True)  31.7 us
    all_gather x1, blocking collectives, on_device(): here = lax.all_gather(piece, 'rows', axis_index_groups=same_core)  30.6 us
    all_to_all x1, blocking collectives, on_device(): lax.all_to_all(jnp.broadcast_to(summed[None], (n_mem, n_gram, p)), 'mem',...  27.5 us
    pallas_call x1, Pallas kernels, prepare(): pl.pallas_call(prepare_kernel, out_shape=[jax.ShapeDtypeStruct((3 * p, lo...  16.5 us
    all_to_all x1, starting transfers between devices, on_device(): got = lax.all_to_all(out, 'rows', 0, 0, tiled=True)  15.5 us
  transfers between devices with their start and end apart: 5, of which 5 were waited for; matrix products, arithmetic and copies ran while one was open for 1% of the time, Pallas kernels for 17%

commit v1 on v0

--- a/solution.py
+++ b/solution.py
@@ -197,9 +197,49 @@
     )(core, here, there, dev, r, e)
 
 
-def prepare_kernel(core_ref, here_ref, there_ref, state_ref, pred_ref, inno_ref, cross_x_ref, cross_h_ref, pay_ref, y_ref):
+def pair(x, axis, order):
+    hi = x.astype(jnp.bfloat16)
+    low = (x - hi.astype(jnp.float32)).astype(jnp.bfloat16)
+    return jnp.concatenate([(hi, low)[k] for k in order], axis=axis)
+
+
+LEFT, RIGHT = (0, 0, 1), (0, 1, 0)
+
+
+def dot3_nt(left, right):
+    return lax.dot_general(left, right, (((1,), (1,)), ((), ())), preferred_element_type=jnp.float32)
+
+
+def pick_kernel(row_ref, owners_ref, positions_ref, pred_ref, pert_ref, out_ref):
+    part = out_ref.shape[1] // 2
+    row = row_ref[0]
+    mine = jnp.where(owners_ref[1] == row, 1, jnp.where(owners_ref[2] == row, 2, 0))
+
+    def step(dest, _):
+        for j in range(part):
+            at = positions_ref[mine, dest * part + j]
+            out_ref[dest, j : j + 1, :] = pred_ref[pl.ds(at, 1), :]
+            out_ref[dest, part + j : part + j + 1, :] = pert_ref[pl.ds(at, 1), :]
+        return 0
+
+    lax.fori_loop(0, out_ref.shape[0], step, 0)
+
+
+def pick(row, owners, positions, predicted, perturbed, n_rows):
+    vm, sm = pl.BlockSpec(memory_space=pltpu.VMEM), pl.BlockSpec(memory_space=pltpu.SMEM)
+    shape = (n_rows, 2 * positions.shape[1] // n_rows, predicted.shape[1])
+    return pl.pallas_call(
+        pick_kernel,
+        out_shape=jax.ShapeDtypeStruct(shape, jnp.float32),
+        in_specs=[sm, sm, sm, vm, vm],
+        out_specs=vm,
+        name="pick",
+    )(row, owners, positions, predicted, perturbed)
+
+
+def cross_kernel(core_ref, here_ref, there_ref, state_ref, pred_ref, inno_ref, y_ref, extra_ref, cross_x_ref, cross_h_ref, right_ref):
     p, local = inno_ref.shape[0] // 3, inno_ref.shape[1]
-    n_mem, part = pay_ref.shape[0], here_ref.shape[2] // 2
+    part = here_ref.shape[2] // 2
     first = core_ref[0] == 0
     for b in range(3):
         mine, other = here_ref[:, b], there_ref[:, b]
@@ -213,28 +253,65 @@
         if b < 2:
             y_ref[(3 + b) * p : (4 + b) * p, :] = inno
     ones = jnp.ones((TILE, local), jnp.float32)
-    n_gram = 6 * p // n_mem
-    row = n_gram
-
-    def extra(values):
-        nonlocal row
+    row = 0
+    extra_ref[...] = jnp.zeros(extra_ref.shape, jnp.float32)
+    for source, factor in ((y_ref, 1.0 / local), (state_ref, 1.0), (pred_ref, 1.0)):
+        values = mm_nt(ones, source[...]) * factor
         for at in range(0, values.shape[1], p):
-            piece = values[0:1, at : at + p]
-            if piece.shape[1] < p:
-                piece = jnp.concatenate([piece, jnp.zeros((1, p - piece.shape[1]), jnp.float32)], axis=1)
-            pay_ref[:, row : row + 1, :] = jnp.broadcast_to(piece[None], (n_mem, 1, p))
+            size = min(p, values.shape[1] - at)
+            extra_ref[row : row + 1, 0:size] = values[0:1, at : at + size]
             row += 1
-
-    pay_ref[:, n_gram:, :] = jnp.zeros((n_mem, pay_ref.shape[1] - n_gram, p), jnp.float32)
-    extra(mm_nt(ones, y_ref[...]) * (1.0 / local))
-    extra(jnp.concatenate([mm_nt(ones, state_ref[...]), mm_nt(ones, pred_ref[...])], axis=1))
     for i in range(5):
         rows = y_ref[i * p : (i + 1) * p, :]
-        y_ref[i * p : (i + 1) * p, :] = rows - jnp.sum(rows, axis=1, keepdims=True) * (1.0 / local)
+        rows = rows - jnp.sum(rows, axis=1, keepdims=True) * (1.0 / local)
+        y_ref[i * p : (i + 1) * p, :] = rows
+        right_ref[i * p : (i + 1) * p, :] = pair(rows, 1, RIGHT)
+    chunk = 128
+    for src_ref, out_ref in ((state_ref, cross_x_ref), (pred_ref, cross_h_ref)):
+
+        def step(n, _, src_ref=src_ref, out_ref=out_ref):
+            at = pl.ds(pl.multiple_of(n * chunk, chunk), chunk)
+            out_ref[at, :] = dot3_nt(pair(src_ref[at, :], 1, LEFT), right_ref[...])
+            return 0
+
+        lax.fori_loop(0, src_ref.shape[0] // chunk, step, 0)
+
+
+def extra_rows(p, *lengths):
+    n = sum(-(-k // p) for k in lengths)
+    return -(-n // TILE) * TILE
+
+
+def cross_products(core, here, there, state, predicted):
+    p, local = here.shape[0] * here.shape[2], state.shape[1]
+    n_x, n_h = state.shape[0], predicted.shape[0]
+    f32 = lambda *shape: jax.ShapeDtypeStruct(shape, jnp.float32)
+    vm = pl.BlockSpec(memory_space=pltpu.VMEM)
+    return pl.pallas_call(
+        cross_kernel,
+        out_shape=[
+            f32(3 * p, local),
+            f32(5 * p, local),
+            f32(extra_rows(p, 5 * p, n_x, n_h), p),
+            f32(n_x, 5 * p),
+            f32(n_h, 5 * p),
+        ],
+        in_specs=[pl.BlockSpec(memory_space=pltpu.SMEM)] + [vm] * 4,
+        out_specs=[vm] * 5,
+        scratch_shapes=[pltpu.VMEM((5 * p, 3 * local), jnp.bfloat16)],
+        name="cross",
+    )(core, here, there, state, predicted)
+
+
+def gram_kernel(core_ref, y_ref, extra_ref, pay_ref):
+    n_mem, p = pay_ref.shape[0], pay_ref.shape[2]
+    n_gram = 6 * p // n_mem
+    pay_ref[:, n_gram:, :] = jnp.broadcast_to(extra_ref[...][None], (n_mem, *extra_ref.shape))
 
     def products(pairs):
         for n, (i, j) in enumerate(pairs):
-            block = mm_nt(y_ref[i * p : (i + 1) * p, :], y_ref[j * p : (j + 1) * p, :])
+            left = pair(y_ref[i * p : (i + 1) * p, :], 1, LEFT)
+            block = dot3_nt(left, pair(y_ref[j * p : (j + 1) * p, :], 1, RIGHT))
             at = 0
             while at < p:
                 dest, off = divmod(n * p + at, n_gram)
@@ -242,43 +319,77 @@
                 pay_ref[dest, off : off + size, :] = block[at : at + size]
                 at += size
 
-    @pl.when(first)
+    @pl.when(core_ref[0] == 0)
     def _():
         products(HALF_A)
 
-    @pl.when(jnp.logical_not(first))
+    @pl.when(core_ref[0] != 0)
     def _():
         products(HALF_B)
 
-    for src_ref, out_ref in ((state_ref, cross_x_ref), (pred_ref, cross_h_ref)):
-        chunk = 128
-
-        def step(n, _, src_ref=src_ref, out_ref=out_ref):
-            at = pl.ds(pl.multiple_of(n * chunk, chunk), chunk)
-            out_ref[at, :] = mm_nt(src_ref[at, :], y_ref[...])
-            return 0
-
-        lax.fori_loop(0, src_ref.shape[0] // chunk, step, 0)
-
-
-def prepare(core, here, there, state, predicted, n_mem):
-    p, local = here.shape[0] * here.shape[2], state.shape[1]
-    n_gram = 6 * p // n_mem
-    n_extra = 5 + -(-(state.shape[0] + predicted.shape[0]) // p)
+
+def gram_payload(core, y, extra, n_mem):
+    p = extra.shape[1]
     vm = pl.BlockSpec(memory_space=pltpu.VMEM)
     return pl.pallas_call(
-        prepare_kernel,
+        gram_kernel,
+        out_shape=jax.ShapeDtypeStruct((n_mem, 6 * p // n_mem + extra.shape[0], p), jnp.float32),
+        in_specs=[pl.BlockSpec(memory_space=pltpu.SMEM), vm, vm],
+        out_specs=vm,
+        name="gram",
+    )(core, y, extra)
+
+
+def update_kernel(steps_x, state_ref, pred_ref, cross_x_ref, cross_h_ref, sums_ref, dev_ref, v_ref, new_x_ref, new_h_ref, right_ref, between_ref):
+    n = pl.program_id(0)
+
+    @pl.when(n == 0)
+    def _():
+        right_ref[...] = pair(v_ref[...], 0, RIGHT)
+        between_ref[...] = mm(dev_ref[...], v_ref[...])
+
+    def one(old_ref, cross_ref, new_ref):
+        step = lax.dot_general(
+            pair(cross_ref[...], 1, LEFT), right_ref[...], (((1,), (0,)), ((), ())), preferred_element_type=jnp.float32
+        )
+        new_ref[...] = old_ref[...] + (step + tn_narrow(sums_ref[...], between_ref[...]))
+
+    @pl.when(n < steps_x)
+    def _():
+        one(state_ref, cross_x_ref, new_x_ref)
+
+    @pl.when(n >= steps_x)
+    def _():
+        one(pred_ref, cross_h_ref, new_h_ref)
+
+
+def update(state, predicted, cross_x, cross_h, sums, dev, v):
+    chunk = 128
+    local, wide = state.shape[1], cross_x.shape[1]
+    steps_x, steps_h = state.shape[0] // chunk, predicted.shape[0] // chunk
+    at_x = lambda n: (jnp.minimum(n, steps_x - 1), 0)
+    at_h = lambda n: (jnp.maximum(n - steps_x, 0), 0)
+    whole = lambda n: (0, 0)
+    return pl.pallas_call(
+        functools.partial(update_kernel, steps_x),
+        grid=(steps_x + steps_h,),
         out_shape=[
-            jax.ShapeDtypeStruct((3 * p, local), jnp.float32),
-            jax.ShapeDtypeStruct((state.shape[0], 5 * p), jnp.float32),
-            jax.ShapeDtypeStruct((predicted.shape[0], 5 * p), jnp.float32),
-            jax.ShapeDtypeStruct((n_mem, n_gram + -(-n_extra // TILE) * TILE, p), jnp.float32),
+            jax.ShapeDtypeStruct(state.shape, jnp.float32),
+            jax.ShapeDtypeStruct(predicted.shape, jnp.float32),
         ],
-        in_specs=[pl.BlockSpec(memory_space=pltpu.SMEM)] + [vm] * 4,
-        out_specs=[vm] * 4,
-        scratch_shapes=[pltpu.VMEM((5 * p, local), jnp.float32)],
-        name="prepare",
-    )(core, here, there, state, predicted)
+        in_specs=[
+            pl.BlockSpec((chunk, local), at_x),
+            pl.BlockSpec((chunk, local), at_h),
+            pl.BlockSpec((chunk, wide), at_x),
+            pl.BlockSpec((chunk, wide), at_h),
+            pl.BlockSpec((sums.shape[0], chunk), lambda n: (0, n)),
+            pl.BlockSpec(dev.shape, whole),
+            pl.BlockSpec(v.shape, whole),
+        ],
+        out_specs=[pl.BlockSpec((chunk, local), at_x), pl.BlockSpec((chunk, local), at_h)],
+        scratch_shapes=[pltpu.VMEM((3 * wide, local), jnp.bfloat16), pltpu.VMEM((dev.shape[0], local), jnp.float32)],
+        name="update",
+    )(state, predicted, cross_x, cross_h, sums, dev, v)
 
 
 def make(n_rows, n_mem):
@@ -291,33 +402,27 @@
         p = positions.shape[1]
         local = state.shape[1]
         members = local * n_mem
-        part = p // n_rows
         row = lax.axis_index("rows")
         core = row % cores
 
-        mine = jnp.argmax(owners == row)
-        picked = positions[mine]
-        out = jnp.concatenate(
-            [
-                jnp.take(predicted, picked, axis=0).reshape(n_rows, part, local),
-                jnp.take(perturbed, picked, axis=0).reshape(n_rows, part, local),
-            ],
-            axis=1,
-        )
+        which = core.reshape(1).astype(jnp.int32)
+        out = pick(row.reshape(1).astype(jnp.int32), owners, positions, predicted, perturbed, n_rows)
         got = lax.all_to_all(out, "rows", 0, 0, tiled=True)
         piece = jnp.take(got, owners, axis=0)
         here = lax.all_gather(piece, "rows", axis_index_groups=same_core)
         there = lax.ppermute(here, "rows", swap)
-        which = core.reshape(1).astype(jnp.int32)
-        inno, cross_x, cross_h, payload = prepare(which, here, there, state, predicted, n_mem)
+        inno, y, extra, cross_x, cross_h = cross_products(which, here, there, state, predicted)
         n_gram = 6 * p // n_mem
-        n_state = state.shape[0] + predicted.shape[0]
         cross_x, cross_h = lax.psum((cross_x, cross_h), "mem")
+        payload = gram_payload(which, y, extra, n_mem)
         got = lax.all_to_all(payload, "mem", 0, 0, tiled=True)
         summed = jnp.sum(got[:, :n_gram], axis=0)
         extra = got[:, n_gram:].reshape(n_mem, -1)
         mu_all = extra[:, : 5 * p]
-        sums_all = extra[:, 5 * p : 5 * p + n_state]
+        n_x = -(-state.shape[0] // p) * p
+        sums_all = jnp.concatenate(
+            [extra[:, 5 * p : 5 * p + state.shape[0]], extra[:, 5 * p + n_x : 5 * p + n_x + predicted.shape[0]]], axis=1
+        )
         here = lax.all_to_all(
             jnp.broadcast_to(summed[None], (n_mem, n_gram, p)), "mem", 0, 0, tiled=True
         ).reshape(6 * p, p)
@@ -333,11 +438,7 @@
             float(local),
             1.0 / (members - 1),
         )
-        between = mm(dev, v)
-        n_x = state.shape[0]
-        new_state = state + mm(cross_x, v) + mm_tn(sums_all[:, :n_x], between)
-        new_obs = predicted + mm(cross_h, v) + mm_tn(sums_all[:, n_x:], between)
-        return new_state, new_obs
+        return update(state, predicted, cross_x, cross_h, sums_all, dev, v)
 
     return on_device
 

time: 293 us -> 288 us (0.983)
  matrix products: 10.4 us -> 0 us
  Pallas kernels: 65.9 us -> 75.6 us
  local copies, waits for them, and re-layouts: 6.64 us -> 3.52 us
    dot_general x5 -> x0, matrix products: 10.4 us -> none  [the longest x3 9.28 us: mm(): lax.dot_general(a, b, (((1,), (0,)), ((), ())), precision=exact, preferre...]
    pallas_call x1 -> x4, Pallas kernels: 16.5 us -> 26.5 us  [the longest x1 11.2 us: cross_products(): pl.pallas_call(cross_kernel, out_shape=[f32(3 * p, local), f32(5 * p, loc...]
    psum x1, waiting for transfers between devices: 33.9 us -> 37.4 us  [on_device(): cross_x, cross_h = lax.psum((cross_x, cross_h), 'mem')]
    gather x2 -> x0, local copies, waits for them, and re-layouts: 2.93 us -> none  [the longest x1 1.96 us: on_device(): jnp.take(predicted, picked, axis=0).reshape(n_rows, part, local)]
where the time goes in v1:
time: 288 us; the launch traced here: 287 us
  waiting for transfers between devices  107 us (37%)
  Pallas kernels  75.6 us (26%)
  blocking collectives  58.3 us (20%)
  starting transfers between devices  26.9 us (9%)
  between operations  14.2 us (5%)
  local copies, waits for them, and re-layouts  3.52 us (1%)
    pallas_call x1, Pallas kernels, chain(): pl.pallas_call(functools.partial(chain_kernel, local, scale), out_shape=j...  49.2 us
    psum x1, waiting for transfers between devices, on_device(): cross_x, cross_h = lax.psum((cross_x, cross_h), 'mem')  37.4 us
    all_to_all x1, waiting for transfers between devices, on_device(): got = lax.all_to_all(out, 'rows', 0, 0, tiled=True)  33.7 us
    all_to_all x1, waiting for transfers between devices, on_device(): got = lax.all_to_all(payload, 'mem', 0, 0, tiled=True)  31.4 us
    all_gather x1, blocking collectives, on_device(): here = lax.all_gather(piece, 'rows', axis_index_groups=same_core)  30.6 us
    all_to_all x1, blocking collectives, on_device(): lax.all_to_all(jnp.broadcast_to(summed[None], (n_mem, n_gram, p)), 'mem',...  27.7 us
    all_to_all x1, starting transfers between devices, on_device(): got = lax.all_to_all(out, 'rows', 0, 0, tiled=True)  15.5 us
    pallas_call x1, Pallas kernels, cross_products(): pl.pallas_call(cross_kernel, out_shape=[f32(3 * p, local), f32(5 * p, loc...  11.2 us
  transfers between devices with their start and end apart: 5, of which 5 were waited for; matrix products, arithmetic and copies ran while one was open for 1% of the time, Pallas kernels for 17%

profile of v1, /device:TPU:6, one launch (start us, length us, event | category | flops | bytes accessed | tf_op | source)
XLA Modules:
  0.0 286.5 jit_solution(2142380329685776753)
XLA Ops:
  7.2 0.0 copy-start.4
  7.2 3.1 %pick.1 = f32[32,16,256]{2,1,0:T(8,128)} custom-call(s32[1]{0:T(128)} %bitcast.1.row_ref, s32[3]{0:T(128)} %owners_ref.1, s32[3,256]{1,0:T(4,128)} %positions_ref.1, f32[384,256]{1,0:T(8,128)} %pred_ref.5, f32[384,256]{1,0:T(8,128)} %pert_ref.1), custom_call_target="tpu_custom_call" | custom-call | tf_op jit(solution)/shard_map/pick/pallas_call | solution.py:231
  10.3 15.5 %all-to-all-start = ((f32[32,16,256]{2,1,0:T(8,128)}), f32[32,16,256]{2,1,0:T(8,128)S(1)}, u32[]{:S(2)}, u32[]{:S(2)}) async-start(f32[32,16,256]{2,1,0:T(8,128)} %pick.1), calls=%async_computation | async-start | bytes 1048576 | tf_op jit(solution)/shard_map/all_to_all | solution.py:410
  25.8 0.0 copy-done.4
  25.9 33.7 %all-to-all-done = f32[32,16,256]{2,1,0:T(8,128)S(1)} async-done(((f32[32,16,256]{2,1,0:T(8,128)}), f32[32,16,256]{2,1,0:T(8,128)S(1)}, u32[]{:S(2)}, u32[]{:S(2)}) %all-to-all-start) | async-done | bytes 524320 | tf_op jit(solution)/shard_map/all_to_all | solution.py:410
  59.6 0.6 gather_fusion
  60.1 0.1 bitcast_select_fusion
  60.2 30.6 %all_gather.4.here_ref = f32[16,3,16,256]{3,2,1,0:T(8,128)S(1)} all-gather(f32[1,3,16,256]{3,2,1,0:T(8,128)S(1)} %bitcast_select_fusion), channel_id=1, replica_groups={{0,32,64,96,128,160,192,224,256,288,320,352,384,416,448,480},{16,48,80,..., dimensions={0}, use_global_device_ids=true | all-gather | bytes 835584 | tf_op jit(solution)/shard_map/all_gather | solution.py:412
  90.8 0.0 copy-start.1
  90.8 1.9 collective-permute-start
  92.8 2.2 collective-permute-done.there_ref
  95.0 0.0 copy-done.1
  95.0 0.9 copy-done.3
  95.9 11.2 %cross.1 = (f32[768,256]{1,0:T(8,128)}, f32[1280,256]{1,0:T(8,128)}, f32[16,256]{1,0:T(8,128)}, f32[512,1280]{1,0:T(8,128)}, f32[384,1280]{1,0:T(8,128)}) custom-call(s32[1]{0:T(128)} %bitcast.core_ref, f32[16,3,16,256]{3,2,1,0:T(8,128)} %copy-done.1, f32[16,3,16,256]{3,2,1,0:T(8,128)} %copy-done.3, f32[512,256]{1,0:T(8,128)} %state_ref.3, f32[384,256]{1,0:T(8,128)} %pred_ref.5), custom_call_target="tpu_custom_call" | custom-call | tf_op jit(solution)/shard_map/cross/pallas_call | solution.py:290
  107.1 3.4 %gram.1 = f32[16,112,256]{2,1,0:T(8,128)} custom-call(s32[1]{0:T(128)} %bitcast.core_ref, f32[1280,256]{1,0:T(8,128)} %get-tuple-element.9.y_ref, f32[16,256]{1,0:T(8,128)} %get-tuple-element.10.extra_ref), custom_call_target="tpu_custom_call" | custom-call | tf_op jit(solution)/shard_map/gram/pallas_call | solution.py:334
  110.5 7.4 %all-to-all-start.1 = ((f32[16,112,256]{2,1,0:T(8,128)}), f32[16,112,256]{2,1,0:T(8,128)S(1)}, u32[]{:S(2)}, u32[]{:S(2)}) async-start(f32[16,112,256]{2,1,0:T(8,128)} %gram.1), calls=%async_computation.1 | async-start | bytes 3670016 | tf_op jit(solution)/shard_map/all_to_all | solution.py:418
  117.9 0.0 all-reduce.3.cloned.1.call-start
  117.9 0.7 all-reduce.3.cloned.1.call-update
  118.6 31.4 %all-to-all-done.1 = f32[16,112,256]{2,1,0:T(8,128)S(1)} async-done(((f32[16,112,256]{2,1,0:T(8,128)}), f32[16,112,256]{2,1,0:T(8,128)S(1)}, u32[]{:S(2)}, u32[]{:S(2)}) %all-to-all-start.1) | async-done | bytes 1835040 | tf_op jit(solution)/shard_map/all_to_all | solution.py:418
  150.0 0.1 slice_reduce_fusion
  150.1 0.1 broadcast_in_dim.22
  150.2 27.7 %all_to_all.15 = f32[16,96,256]{2,1,0:T(8,128)S(1)} all-to-all(f32[16,96,256]{2,1,0:T(8,128)S(1)} %broadcast_in_dim.22), channel_id=1, replica_groups=mesh['rows'=32,'mem'=16] {'mem'}, dimensions={0} | all-to-all | bytes 3145728 | tf_op jit(solution)/shard_map/all_to_all | solution.py:426
  177.9 2.1 collective-permute-start.1
  180.1 0.2 copy.8
  180.2 0.6 concatenate.4.sums_ref
  180.9 0.6 slice_subtract_fusion.dev_ref
  181.5 1.7 collective-permute-done.1.there_ref
  183.2 1.1 copy-done.2
  184.4 0.0 copy-done
  184.4 49.2 %chain.1.v_ref = f32[1280,256]{1,0:T(8,128)} custom-call(s32[1]{0:T(128)} %bitcast.core_ref, f32[1536,256]{1,0:T(8,128)} %bitcast.8, f32[1536,256]{1,0:T(8,128)} %copy-done.2, f32[16,1280]{1,0:T(8,128)} %slice_subtract_fusion.dev_ref, f32[3,256]{1,0:T(4,128)} %r_ref.1, f32[768,256]{1,0:T(8,128)} %get-tuple-element.11.e_ref), custom_call_target="tpu_custom_call" | custom-call | tf_op jit(solution)/shard_map/chain/pallas_call | solution.py:189
  233.5 37.4 %all-reduce.3.cloned.1.call-done = (f32[512,1280]{1,0:T(8,128)}, f32[384,1280]{1,0:T(8,128)}) async-done(((f32[512,1280]{1,0:T(8,128)}, f32[384,1280]{1,0:T(8,128)}), (f32[512,1280]{1,0:T(8,128)}, f32[384,1280]{1,0:T(8,128)})) %all-reduce.3.cloned.1.call-update) | async-done | bytes 4587536 | tf_op jit(solution)/shard_map/psum | solution.py:416
  270.9 8.8 %update.1 = (f32[512,256]{1,0:T(8,128)}, f32[384,256]{1,0:T(8,128)}) custom-call(f32[512,256]{1,0:T(8,128)} %state_ref.3, f32[384,256]{1,0:T(8,128)} %pred_ref.5, f32[512,1280]{1,0:T(8,128)} %get-tuple-element.12.cross_x_ref, f32[384,1280]{1,0:T(8,128)} %get-tuple-element.13.cross_h_ref, f32[16,896]{1,0:T(8,128)} %concatenate.4.sums_ref, ...), custom_call_target="tpu_custom_call" | custom-call | tf_op jit(solution)/shard_map/update/pallas_call | solution.py:373
  (9 shorter events, 0.1 us)
Async XLA Ops:
  7.2 18.6 %copy-start.4 = (s32[3]{0:T(128)S(1)}, s32[3]{0:T(128)}, u32[]{:S(2)}) copy-start(s32[3]{0:T(128)} %owners_ref.1) | copy-start | bytes 40
  10.3 49.3 %all-to-all-start = ((f32[32,16,256]{2,1,0:T(8,128)}), f32[32,16,256]{2,1,0:T(8,128)S(1)}, u32[]{:S(2)}, u32[]{:S(2)}) async-start(f32[32,16,256]{2,1,0:T(8,128)} %pick.1), calls=%async_computation | async-start | bytes 1048576 | tf_op jit(solution)/shard_map/all_to_all | solution.py:410
  90.8 4.2 %copy-start.1 = (f32[16,3,16,256]{3,2,1,0:T(8,128)}, f32[16,3,16,256]{3,2,1,0:T(8,128)S(1)}, u32[]{:S(2)}) copy-start(f32[16,3,16,256]{3,2,1,0:T(8,128)S(1)} %all_gather.4.here_ref) | copy-start | bytes 2359300
  90.8 4.2 %collective-permute-start = (f32[16,3,16,256]{3,2,1,0:T(8,128)S(1)}, f32[16,3,16,256]{3,2,1,0:T(8,128)S(1)}, u32[]{:S(2)}, u32[]{:S(2)}) collective-permute-start(f32[16,3,16,256]{3,2,1,0:T(8,128)S(1)} %all_gather.4.here_ref), channel_id=1, source_target_pairs={{0,16},{16,0},{32,48},{48,32},{64,80},{80,64},{96,112},{112,96},{1... | collective-permute-start | bytes 2359304 | tf_op jit(solution)/shard_map/ppermute | solution.py:413
  95.0 0.9 copy-start.3
  110.5 39.5 %all-to-all-start.1 = ((f32[16,112,256]{2,1,0:T(8,128)}), f32[16,112,256]{2,1,0:T(8,128)S(1)}, u32[]{:S(2)}, u32[]{:S(2)}) async-start(f32[16,112,256]{2,1,0:T(8,128)} %gram.1), calls=%async_computation.1 | async-start | bytes 3670016 | tf_op jit(solution)/shard_map/all_to_all | solution.py:418
  117.9 153.0 %all-reduce.3.cloned.1.call-start = ((), (), s32[]{:S(2)}) async-start(), calls=%async_computation.3 | async-start | bytes 9175040 | tf_op jit(solution)/shard_map/psum | solution.py:416
  177.9 6.4 %copy-start = (f32[16,96,256]{2,1,0:T(8,128)}, f32[16,96,256]{2,1,0:T(8,128)S(1)}, u32[]{:S(2)}) copy-start(f32[16,96,256]{2,1,0:T(8,128)S(1)} %all_to_all.15) | copy-start | bytes 4718596
  177.9 5.3 %collective-permute-start.1 = (f32[1536,256]{1,0:T(8,128)S(1)}, f32[1536,256]{1,0:T(8,128)S(1)}, u32[]{:S(2)}, u32[]{:S(2)}) collective-permute-start(f32[1536,256]{1,0:T(8,128)S(1)} %bitcast.7), channel_id=1, source_target_pairs={{0,16},{16,0},{32,48},{48,32},{64,80},{80,64},{96,112},{112,96},{1... | collective-permute-start | bytes 4718600 | tf_op jit(solution)/shard_map/ppermute | solution.py:429
  183.2 1.1 copy-start.2
Sparse Core Ops, SparseCore 0:
  122.2 148.6 all-reduce.2

commit v2 on v1

--- a/solution.py
+++ b/solution.py
@@ -204,6 +204,7 @@
 
 
 LEFT, RIGHT = (0, 0, 1), (0, 1, 0)
+STEPS = 2
 
 
 def dot3_nt(left, right):
@@ -237,9 +238,10 @@
     )(row, owners, positions, predicted, perturbed)
 
 
-def cross_kernel(core_ref, here_ref, there_ref, state_ref, pred_ref, inno_ref, y_ref, extra_ref, cross_x_ref, cross_h_ref, right_ref):
+def cross_kernel(core_ref, here_ref, there_ref, state_ref, pred_ref, inno_ref, y_ref, cross_x_ref, cross_h_ref, left_ref, right_ref):
     p, local = inno_ref.shape[0] // 3, inno_ref.shape[1]
     part = here_ref.shape[2] // 2
+    n_x = state_ref.shape[0]
     first = core_ref[0] == 0
     for b in range(3):
         mine, other = here_ref[:, b], there_ref[:, b]
@@ -250,62 +252,61 @@
         inno = pert - obs
         inno_ref[b * p : (b + 1) * p, :] = inno
         y_ref[b * p : (b + 1) * p, :] = obs
+        right_ref[b * p : (b + 1) * p, :] = pair(centred(obs), 1, RIGHT)
         if b < 2:
             y_ref[(3 + b) * p : (4 + b) * p, :] = inno
+            right_ref[(3 + b) * p : (4 + b) * p, :] = pair(centred(inno), 1, RIGHT)
+    left_ref[:n_x, :] = pair(state_ref[...], 1, LEFT)
+    left_ref[n_x:, :] = pair(pred_ref[...], 1, LEFT)
+
+    def step(n, _):
+        at = pl.ds(pl.multiple_of(n * p, p), p)
+        block = dot3_nt(left_ref[...], right_ref[at, :])
+        cross_x_ref[:, at] = block[:n_x]
+        cross_h_ref[:, at] = block[n_x:]
+        return 0
+
+    lax.fori_loop(0, 5, step, 0)
+
+
+def centred(rows):
+    return rows - jnp.sum(rows, axis=1, keepdims=True) * (1.0 / rows.shape[1])
+
+
+def extra_rows(p, *lengths):
+    n = sum(-(-k // p) for k in lengths)
+    return -(-n // TILE) * TILE
+
+
+def cross_products(core, here, there, state, predicted):
+    p, local = here.shape[0] * here.shape[2], state.shape[1]
+    n_x, n_h = state.shape[0], predicted.shape[0]
+    f32 = lambda *shape: jax.ShapeDtypeStruct(shape, jnp.float32)
+    vm = pl.BlockSpec(memory_space=pltpu.VMEM)
+    return pl.pallas_call(
+        cross_kernel,
+        out_shape=[f32(3 * p, local), f32(5 * p, local), f32(n_x, 5 * p), f32(n_h, 5 * p)],
+        in_specs=[pl.BlockSpec(memory_space=pltpu.SMEM)] + [vm] * 4,
+        out_specs=[vm] * 4,
+        scratch_shapes=[pltpu.VMEM((n_x + n_h, 3 * local), jnp.bfloat16), pltpu.VMEM((5 * p, 3 * local), jnp.bfloat16)],
+        name="cross",
+    )(core, here, there, state, predicted)
+
+
+def gram_kernel(core_ref, raw_ref, state_ref, pred_ref, pay_ref, y_ref, extra_ref):
+    n_mem, p, local = pay_ref.shape[0], pay_ref.shape[2], raw_ref.shape[1]
+    n_gram = 6 * p // n_mem
     ones = jnp.ones((TILE, local), jnp.float32)
     row = 0
     extra_ref[...] = jnp.zeros(extra_ref.shape, jnp.float32)
-    for source, factor in ((y_ref, 1.0 / local), (state_ref, 1.0), (pred_ref, 1.0)):
+    for source, factor in ((raw_ref, 1.0 / local), (state_ref, 1.0), (pred_ref, 1.0)):
         values = mm_nt(ones, source[...]) * factor
         for at in range(0, values.shape[1], p):
             size = min(p, values.shape[1] - at)
             extra_ref[row : row + 1, 0:size] = values[0:1, at : at + size]
             row += 1
     for i in range(5):
-        rows = y_ref[i * p : (i + 1) * p, :]
-        rows = rows - jnp.sum(rows, axis=1, keepdims=True) * (1.0 / local)
-        y_ref[i * p : (i + 1) * p, :] = rows
-        right_ref[i * p : (i + 1) * p, :] = pair(rows, 1, RIGHT)
-    chunk = 128
-    for src_ref, out_ref in ((state_ref, cross_x_ref), (pred_ref, cross_h_ref)):
-
-        def step(n, _, src_ref=src_ref, out_ref=out_ref):
-            at = pl.ds(pl.multiple_of(n * chunk, chunk), chunk)
-            out_ref[at, :] = dot3_nt(pair(src_ref[at, :], 1, LEFT), right_ref[...])
-            return 0
-
-        lax.fori_loop(0, src_ref.shape[0] // chunk, step, 0)
-
-
-def extra_rows(p, *lengths):
-    n = sum(-(-k // p) for k in lengths)
-    return -(-n // TILE) * TILE
-
-
-def cross_products(core, here, there, state, predicted):
-    p, local = here.shape[0] * here.shape[2], state.shape[1]
-    n_x, n_h = state.shape[0], predicted.shape[0]
-    f32 = lambda *shape: jax.ShapeDtypeStruct(shape, jnp.float32)
-    vm = pl.BlockSpec(memory_space=pltpu.VMEM)
-    return pl.pallas_call(
-        cross_kernel,
-        out_shape=[
-            f32(3 * p, local),
-            f32(5 * p, local),
-            f32(extra_rows(p, 5 * p, n_x, n_h), p),
-            f32(n_x, 5 * p),
-            f32(n_h, 5 * p),
-        ],
-        in_specs=[pl.BlockSpec(memory_space=pltpu.SMEM)] + [vm] * 4,
-        out_specs=[vm] * 5,
-        scratch_shapes=[pltpu.VMEM((5 * p, 3 * local), jnp.bfloat16)],
-        name="cross",
-    )(core, here, there, state, predicted)
-
-
-def gram_kernel(core_ref, y_ref, extra_ref, pay_ref):
-    n_mem, p = pay_ref.shape[0], pay_ref.shape[2]
-    n_gram = 6 * p // n_mem
+        y_ref[i * p : (i + 1) * p, :] = centred(raw_ref[i * p : (i + 1) * p, :])
     pay_ref[:, n_gram:, :] = jnp.broadcast_to(extra_ref[...][None], (n_mem, *extra_ref.shape))
 
     def products(pairs):
@@ -328,68 +329,83 @@
         products(HALF_B)
 
 
-def gram_payload(core, y, extra, n_mem):
-    p = extra.shape[1]
+def gram_payload(core, y, state, predicted, p, n_mem):
+    n_extra = extra_rows(p, y.shape[0], state.shape[0], predicted.shape[0])
     vm = pl.BlockSpec(memory_space=pltpu.VMEM)
     return pl.pallas_call(
         gram_kernel,
-        out_shape=jax.ShapeDtypeStruct((n_mem, 6 * p // n_mem + extra.shape[0], p), jnp.float32),
-        in_specs=[pl.BlockSpec(memory_space=pltpu.SMEM), vm, vm],
+        out_shape=jax.ShapeDtypeStruct((n_mem, 6 * p // n_mem + n_extra, p), jnp.float32),
+        in_specs=[pl.BlockSpec(memory_space=pltpu.SMEM), vm, vm, vm],
         out_specs=vm,
+        scratch_shapes=[pltpu.VMEM(y.shape, jnp.float32), pltpu.VMEM((n_extra, p), jnp.float32)],
         name="gram",
-    )(core, y, extra)
-
-
-def update_kernel(steps_x, state_ref, pred_ref, cross_x_ref, cross_h_ref, sums_ref, dev_ref, v_ref, new_x_ref, new_h_ref, right_ref, between_ref):
-    n = pl.program_id(0)
-
-    @pl.when(n == 0)
+    )(core, y, state, predicted)
+
+
+def base_kernel(state_ref, pred_ref, sums_ref, dev_ref, v_ref, base_x_ref, base_h_ref, right_ref):
+    n_x = state_ref.shape[0]
+    wide = v_ref.shape[0] // STEPS
+    dev = pair(dev_ref[...], 1, LEFT)
+    right = pair(v_ref[...], 0, RIGHT)
+    between = lax.dot_general(dev, right, (((1,), (0,)), ((), ())), preferred_element_type=jnp.float32)
+    between = tn_narrow(sums_ref[...], between)
+    base_x_ref[...] = state_ref[...] + between[:n_x]
+    base_h_ref[...] = pred_ref[...] + between[n_x:]
+    for n in range(STEPS):
+        right_ref[3 * n * wide : 3 * (n + 1) * wide, :] = pair(v_ref[n * wide : (n + 1) * wide, :], 0, RIGHT)
+
+
+def update_kernel(base_x_ref, base_h_ref, cross_x_ref, cross_h_ref, right_ref, new_x_ref, new_h_ref):
+    n_x = base_x_ref.shape[0]
+
+    @pl.when(pl.program_id(0) == 0)
     def _():
-        right_ref[...] = pair(v_ref[...], 0, RIGHT)
-        between_ref[...] = mm(dev_ref[...], v_ref[...])
-
-    def one(old_ref, cross_ref, new_ref):
-        step = lax.dot_general(
-            pair(cross_ref[...], 1, LEFT), right_ref[...], (((1,), (0,)), ((), ())), preferred_element_type=jnp.float32
-        )
-        new_ref[...] = old_ref[...] + (step + tn_narrow(sums_ref[...], between_ref[...]))
-
-    @pl.when(n < steps_x)
-    def _():
-        one(state_ref, cross_x_ref, new_x_ref)
-
-    @pl.when(n >= steps_x)
-    def _():
-        one(pred_ref, cross_h_ref, new_h_ref)
-
-
-def update(state, predicted, cross_x, cross_h, sums, dev, v):
-    chunk = 128
-    local, wide = state.shape[1], cross_x.shape[1]
-    steps_x, steps_h = state.shape[0] // chunk, predicted.shape[0] // chunk
-    at_x = lambda n: (jnp.minimum(n, steps_x - 1), 0)
-    at_h = lambda n: (jnp.maximum(n - steps_x, 0), 0)
-    whole = lambda n: (0, 0)
-    return pl.pallas_call(
-        functools.partial(update_kernel, steps_x),
-        grid=(steps_x + steps_h,),
+        new_x_ref[...] = base_x_ref[...]
+        new_h_ref[...] = base_h_ref[...]
+
+    left = jnp.concatenate([pair(cross_x_ref[...], 1, LEFT), pair(cross_h_ref[...], 1, LEFT)], axis=0)
+    step = lax.dot_general(left, right_ref[...], (((1,), (0,)), ((), ())), preferred_element_type=jnp.float32)
+    new_x_ref[...] = new_x_ref[...] + step[:n_x]
+    new_h_ref[...] = new_h_ref[...] + step[n_x:]
+
+
+def base_of(state, predicted, sums, dev, v):
+    vm = pl.BlockSpec(memory_space=pltpu.VMEM)
+    return pl.pallas_call(
+        base_kernel,
         out_shape=[
             jax.ShapeDtypeStruct(state.shape, jnp.float32),
             jax.ShapeDtypeStruct(predicted.shape, jnp.float32),
+            jax.ShapeDtypeStruct((3 * v.shape[0], v.shape[1]), jnp.bfloat16),
+        ],
+        in_specs=[vm] * 5,
+        out_specs=[vm] * 3,
+        name="base",
+    )(state, predicted, sums, dev, v)
+
+
+def update(base_x, base_h, cross_x, cross_h, right):
+    local = base_x.shape[1]
+    n_x, n_h = base_x.shape[0], base_h.shape[0]
+    wide = cross_x.shape[1] // STEPS
+    whole = lambda n: (0, 0)
+    return pl.pallas_call(
+        update_kernel,
+        grid=(STEPS,),
+        out_shape=[
+            jax.ShapeDtypeStruct(base_x.shape, jnp.float32),
+            jax.ShapeDtypeStruct(base_h.shape, jnp.float32),
         ],
         in_specs=[
-            pl.BlockSpec((chunk, local), at_x),
-            pl.BlockSpec((chunk, local), at_h),
-            pl.BlockSpec((chunk, wide), at_x),
-            pl.BlockSpec((chunk, wide), at_h),
-            pl.BlockSpec((sums.shape[0], chunk), lambda n: (0, n)),
-            pl.BlockSpec(dev.shape, whole),
-            pl.BlockSpec(v.shape, whole),
+            pl.BlockSpec(base_x.shape, whole),
+            pl.BlockSpec(base_h.shape, whole),
+            pl.BlockSpec((n_x, wide), lambda n: (0, n)),
+            pl.BlockSpec((n_h, wide), lambda n: (0, n)),
+            pl.BlockSpec((3 * wide, local), lambda n: (n, 0)),
         ],
-        out_specs=[pl.BlockSpec((chunk, local), at_x), pl.BlockSpec((chunk, local), at_h)],
-        scratch_shapes=[pltpu.VMEM((3 * wide, local), jnp.bfloat16), pltpu.VMEM((dev.shape[0], local), jnp.float32)],
+        out_specs=[pl.BlockSpec(base_x.shape, whole), pl.BlockSpec(base_h.shape, whole)],
         name="update",
-    )(state, predicted, cross_x, cross_h, sums, dev, v)
+    )(base_x, base_h, cross_x, cross_h, right)
 
 
 def make(n_rows, n_mem):
@@ -411,10 +427,10 @@
         piece = jnp.take(got, owners, axis=0)
         here = lax.all_gather(piece, "rows", axis_index_groups=same_core)
         there = lax.ppermute(here, "rows", swap)
-        inno, y, extra, cross_x, cross_h = cross_products(which, here, there, state, predicted)
+        inno, y, cross_x, cross_h = cross_products(which, here, there, state, predicted)
         n_gram = 6 * p // n_mem
         cross_x, cross_h = lax.psum((cross_x, cross_h), "mem")
-        payload = gram_payload(which, y, extra, n_mem)
+        payload = gram_payload(which, y, state, predicted, p, n_mem)
         got = lax.all_to_all(payload, "mem", 0, 0, tiled=True)
         summed = jnp.sum(got[:, :n_gram], axis=0)
         extra = got[:, n_gram:].reshape(n_mem, -1)
@@ -438,7 +454,8 @@
             float(local),
             1.0 / (members - 1),
         )
-        return update(state, predicted, cross_x, cross_h, sums_all, dev, v)
+        base_x, base_h, right = base_of(state, predicted, sums_all, dev, v)
+        return update(base_x, base_h, cross_x, cross_h, right)
 
     return on_device
 

time: 288 us -> 283 us (0.983)
  waiting for transfers between devices: 107 us -> 103 us
    psum x1, waiting for transfers between devices: 37.4 us -> 33.1 us  [on_device(): cross_x, cross_h = lax.psum((cross_x, cross_h), 'mem')]
    pallas_call x1, Pallas kernels: 11.2 us -> 7.24 us  [cross_products(): pl.pallas_call(cross_kernel, out_shape=[f32(3 * p, local), f32(5 * p, loc...]
    pallas_call x1 -> x2, Pallas kernels: 8.78 us -> 9.65 us  [the longest x1 5.58 us: update(): pl.pallas_call(update_kernel, grid=(STEPS,), out_shape=[jax.ShapeDtypeStr...]
  transfers between devices with their start and end apart: 5 -> 5, of which waited for: 5 -> 5; matrix products, arithmetic and copies ran while one was open for 1% -> 1% of each run, Pallas kernels for 17% -> 19%
where the time goes in v2:
time: 283 us; the launch traced here: 281 us
  waiting for transfers between devices  103 us (36%)
  Pallas kernels  74.9 us (26%)
  blocking collectives  58.3 us (21%)
  starting transfers between devices  26.9 us (10%)
  between operations  14.2 us (5%)
  local copies, waits for them, and re-layouts  3.52 us (1%)
    pallas_call x1, Pallas kernels, chain(): pl.pallas_call(functools.partial(chain_kernel, local, scale), out_shape=j...  49.4 us
    all_to_all x1, waiting for transfers between devices, on_device(): got = lax.all_to_all(out, 'rows', 0, 0, tiled=True)  33.7 us
    psum x1, waiting for transfers between devices, on_device(): cross_x, cross_h = lax.psum((cross_x, cross_h), 'mem')  33.1 us
    all_to_all x1, waiting for transfers between devices, on_device(): got = lax.all_to_all(payload, 'mem', 0, 0, tiled=True)  31.4 us
    all_gather x1, blocking collectives, on_device(): here = lax.all_gather(piece, 'rows', axis_index_groups=same_core)  30.6 us
    all_to_all x1, blocking collectives, on_device(): lax.all_to_all(jnp.broadcast_to(summed[None], (n_mem, n_gram, p)), 'mem',...  27.7 us
    all_to_all x1, starting transfers between devices, on_device(): got = lax.all_to_all(out, 'rows', 0, 0, tiled=True)  15.5 us
    all_to_all x1, starting transfers between devices, on_device(): got = lax.all_to_all(payload, 'mem', 0, 0, tiled=True)  7.43 us
  transfers between devices with their start and end apart: 5, of which 5 were waited for; matrix products, arithmetic and copies ran while one was open for 1% of the time, Pallas kernels for 19%

profile of v2, /device:TPU:6, one launch (start us, length us, event | category | flops | bytes accessed | tf_op | source)
XLA Modules:
  0.0 281.5 jit_solution(99709901296617618)
XLA Ops:
  7.2 0.0 copy-start.4
  7.2 3.1 %pick.1 = f32[32,16,256]{2,1,0:T(8,128)} custom-call(s32[1]{0:T(128)} %bitcast.1.row_ref, s32[3]{0:T(128)} %owners_ref.1, s32[3,256]{1,0:T(4,128)} %positions_ref.1, f32[384,256]{1,0:T(8,128)} %pred_ref.7, f32[384,256]{1,0:T(8,128)} %pert_ref.1), custom_call_target="tpu_custom_call" | custom-call | tf_op jit(solution)/shard_map/pick/pallas_call | solution.py:232
  10.3 15.5 %all-to-all-start = ((f32[32,16,256]{2,1,0:T(8,128)}), f32[32,16,256]{2,1,0:T(8,128)S(1)}, u32[]{:S(2)}, u32[]{:S(2)}) async-start(f32[32,16,256]{2,1,0:T(8,128)} %pick.1), calls=%async_computation | async-start | bytes 1048576 | tf_op jit(solution)/shard_map/all_to_all | solution.py:426
  25.8 0.0 copy-done.4
  25.9 33.7 %all-to-all-done = f32[32,16,256]{2,1,0:T(8,128)S(1)} async-done(((f32[32,16,256]{2,1,0:T(8,128)}), f32[32,16,256]{2,1,0:T(8,128)S(1)}, u32[]{:S(2)}, u32[]{:S(2)}) %all-to-all-start) | async-done | bytes 524320 | tf_op jit(solution)/shard_map/all_to_all | solution.py:426
  59.6 0.6 gather_fusion
  60.1 0.1 bitcast_select_fusion
  60.2 30.6 %all_gather.4.here_ref = f32[16,3,16,256]{3,2,1,0:T(8,128)S(1)} all-gather(f32[1,3,16,256]{3,2,1,0:T(8,128)S(1)} %bitcast_select_fusion), channel_id=1, replica_groups={{0,32,64,96,128,160,192,224,256,288,320,352,384,416,448,480},{16,48,80,..., dimensions={0}, use_global_device_ids=true | all-gather | bytes 835584 | tf_op jit(solution)/shard_map/all_gather | solution.py:428
  90.8 1.9 collective-permute-start
  92.8 2.2 collective-permute-done.there_ref
  95.0 0.0 copy-done.1
  95.0 0.9 copy-done.3
  95.9 7.2 %cross.1 = (f32[768,256]{1,0:T(8,128)}, f32[1280,256]{1,0:T(8,128)}, f32[512,1280]{1,0:T(8,128)}, f32[384,1280]{1,0:T(8,128)}) custom-call(s32[1]{0:T(128)} %bitcast.core_ref, f32[16,3,16,256]{3,2,1,0:T(8,128)} %copy-done.1, f32[16,3,16,256]{3,2,1,0:T(8,128)} %copy-done.3, f32[512,256]{1,0:T(8,128)} %state_ref.5, f32[384,256]{1,0:T(8,128)} %pred_ref.7), custom_call_target="tpu_custom_call" | custom-call | tf_op jit(solution)/shard_map/cross/pallas_call | solution.py:286
  103.1 5.5 %gram.1 = f32[16,112,256]{2,1,0:T(8,128)} custom-call(s32[1]{0:T(128)} %bitcast.core_ref, f32[1280,256]{1,0:T(8,128)} %get-tuple-element.9.raw_ref, f32[512,256]{1,0:T(8,128)} %state_ref.5, f32[384,256]{1,0:T(8,128)} %pred_ref.7), custom_call_target="tpu_custom_call" | custom-call | tf_op jit(solution)/shard_map/gram/pallas_call | solution.py:335
  108.6 7.4 %all-to-all-start.1 = ((f32[16,112,256]{2,1,0:T(8,128)}), f32[16,112,256]{2,1,0:T(8,128)S(1)}, u32[]{:S(2)}, u32[]{:S(2)}) async-start(f32[16,112,256]{2,1,0:T(8,128)} %gram.1), calls=%async_computation.1 | async-start | bytes 3670016 | tf_op jit(solution)/shard_map/all_to_all | solution.py:434
  116.0 0.0 all-reduce.3.cloned.1.call-start
  116.1 0.7 all-reduce.3.cloned.1.call-update
  116.8 31.4 %all-to-all-done.1 = f32[16,112,256]{2,1,0:T(8,128)S(1)} async-done(((f32[16,112,256]{2,1,0:T(8,128)}), f32[16,112,256]{2,1,0:T(8,128)S(1)}, u32[]{:S(2)}, u32[]{:S(2)}) %all-to-all-start.1) | async-done | bytes 1835040 | tf_op jit(solution)/shard_map/all_to_all | solution.py:434
  148.2 0.1 slice_reduce_fusion
  148.3 0.1 broadcast_in_dim.22
  148.4 27.7 %all_to_all.15 = f32[16,96,256]{2,1,0:T(8,128)S(1)} all-to-all(f32[16,96,256]{2,1,0:T(8,128)S(1)} %broadcast_in_dim.22), channel_id=1, replica_groups=mesh['rows'=32,'mem'=16] {'mem'}, dimensions={0} | all-to-all | bytes 3145728 | tf_op jit(solution)/shard_map/all_to_all | solution.py:442
  176.1 2.1 collective-permute-start.1
  178.2 0.2 copy.8
  178.4 0.6 concatenate.4.sums_ref
  179.0 0.6 slice_subtract_fusion.dev_ref
  179.7 1.7 collective-permute-done.1.there_ref
  181.4 1.1 copy-done.2
  182.5 0.0 copy-done
  182.5 49.4 %chain.1.v_ref = f32[1280,256]{1,0:T(8,128)} custom-call(s32[1]{0:T(128)} %bitcast.core_ref, f32[1536,256]{1,0:T(8,128)} %bitcast.8, f32[1536,256]{1,0:T(8,128)} %copy-done.2, f32[16,1280]{1,0:T(8,128)} %slice_subtract_fusion.dev_ref, f32[3,256]{1,0:T(4,128)} %r_ref.1, f32[768,256]{1,0:T(8,128)} %get-tuple-element.10.e_ref), custom_call_target="tpu_custom_call" | custom-call | tf_op jit(solution)/shard_map/chain/pallas_call | solution.py:189
  231.9 4.1 %base.1 = (f32[512,256]{1,0:T(8,128)}, f32[384,256]{1,0:T(8,128)}, bf16[3840,256]{1,0:T(8,128)(2,1)}) custom-call(f32[512,256]{1,0:T(8,128)} %state_ref.5, f32[384,256]{1,0:T(8,128)} %pred_ref.7, f32[16,896]{1,0:T(8,128)} %concatenate.4.sums_ref, f32[16,1280]{1,0:T(8,128)} %slice_subtract_fusion.dev_ref, f32[1280,256]{1,0:T(8,128)} %chain.1.v_ref), custom_call_target="tpu_custom_call" | custom-call | tf_op jit(solution)/shard_map/base/pallas_call | solution.py:374
  235.9 33.1 %all-reduce.3.cloned.1.call-done = (f32[512,1280]{1,0:T(8,128)}, f32[384,1280]{1,0:T(8,128)}) async-done(((f32[512,1280]{1,0:T(8,128)}, f32[384,1280]{1,0:T(8,128)}), (f32[512,1280]{1,0:T(8,128)}, f32[384,1280]{1,0:T(8,128)})) %all-reduce.3.cloned.1.call-update) | async-done | bytes 4587536 | tf_op jit(solution)/shard_map/psum | solution.py:432
  269.1 5.6 %update.1 = (f32[512,256]{1,0:T(8,128)}, f32[384,256]{1,0:T(8,128)}) custom-call(f32[512,256]{1,0:T(8,128)} %get-tuple-element.11.base_x_ref, f32[384,256]{1,0:T(8,128)} %get-tuple-element.12.base_h_ref, f32[512,1280]{1,0:T(8,128)} %get-tuple-element.16.cross_x_ref, f32[384,1280]{1,0:T(8,128)} %get-tuple-element.17.cross_h_ref, ...), custom_call_target="tpu_custom_call" | custom-call | tf_op jit(solution)/shard_map/update/pallas_call | solution.py:392
  (10 shorter events, 0.1 us)
Async XLA Ops:
  7.2 18.6 %copy-start.4 = (s32[3]{0:T(128)S(1)}, s32[3]{0:T(128)}, u32[]{:S(2)}) copy-start(s32[3]{0:T(128)} %owners_ref.1) | copy-start | bytes 40
  10.3 49.3 %all-to-all-start = ((f32[32,16,256]{2,1,0:T(8,128)}), f32[32,16,256]{2,1,0:T(8,128)S(1)}, u32[]{:S(2)}, u32[]{:S(2)}) async-start(f32[32,16,256]{2,1,0:T(8,128)} %pick.1), calls=%async_computation | async-start | bytes 1048576 | tf_op jit(solution)/shard_map/all_to_all | solution.py:426
  90.8 4.2 %copy-start.1 = (f32[16,3,16,256]{3,2,1,0:T(8,128)}, f32[16,3,16,256]{3,2,1,0:T(8,128)S(1)}, u32[]{:S(2)}) copy-start(f32[16,3,16,256]{3,2,1,0:T(8,128)S(1)} %all_gather.4.here_ref) | copy-start | bytes 2359300
  90.8 4.2 %collective-permute-start = (f32[16,3,16,256]{3,2,1,0:T(8,128)S(1)}, f32[16,3,16,256]{3,2,1,0:T(8,128)S(1)}, u32[]{:S(2)}, u32[]{:S(2)}) collective-permute-start(f32[16,3,16,256]{3,2,1,0:T(8,128)S(1)} %all_gather.4.here_ref), channel_id=1, source_target_pairs={{0,16},{16,0},{32,48},{48,32},{64,80},{80,64},{96,112},{112,96},{1... | collective-permute-start | bytes 2359304 | tf_op jit(solution)/shard_map/ppermute | solution.py:429
  95.0 0.9 copy-start.3
  108.6 39.6 %all-to-all-start.1 = ((f32[16,112,256]{2,1,0:T(8,128)}), f32[16,112,256]{2,1,0:T(8,128)S(1)}, u32[]{:S(2)}, u32[]{:S(2)}) async-start(f32[16,112,256]{2,1,0:T(8,128)} %gram.1), calls=%async_computation.1 | async-start | bytes 3670016 | tf_op jit(solution)/shard_map/all_to_all | solution.py:434
  116.0 153.0 %all-reduce.3.cloned.1.call-start = ((), (), s32[]{:S(2)}) async-start(), calls=%async_computation.3 | async-start | bytes 9175040 | tf_op jit(solution)/shard_map/psum | solution.py:432
  176.1 6.4 %copy-start = (f32[16,96,256]{2,1,0:T(8,128)}, f32[16,96,256]{2,1,0:T(8,128)S(1)}, u32[]{:S(2)}) copy-start(f32[16,96,256]{2,1,0:T(8,128)S(1)} %all_to_all.15) | copy-start | bytes 4718596
  176.1 5.3 %collective-permute-start.1 = (f32[1536,256]{1,0:T(8,128)S(1)}, f32[1536,256]{1,0:T(8,128)S(1)}, u32[]{:S(2)}, u32[]{:S(2)}) collective-permute-start(f32[1536,256]{1,0:T(8,128)S(1)} %bitcast.7), channel_id=1, source_target_pairs={{0,16},{16,0},{32,48},{48,32},{64,80},{80,64},{96,112},{112,96},{1... | collective-permute-start | bytes 4718600 | tf_op jit(solution)/shard_map/ppermute | solution.py:445
  181.4 1.1 copy-start.2
Sparse Core Ops, SparseCore 0:
  120.3 148.6 all-reduce.2

commit v3 on v2

--- a/solution.py
+++ b/solution.py
@@ -423,8 +423,15 @@
 
         which = core.reshape(1).astype(jnp.int32)
         out = pick(row.reshape(1).astype(jnp.int32), owners, positions, predicted, perturbed, n_rows)
-        got = lax.all_to_all(out, "rows", 0, 0, tiled=True)
-        piece = jnp.take(got, owners, axis=0)
+        half = out.shape[1]
+        got = lax.all_to_all(
+            out.reshape(n_z, cores * half, local), "rows", 0, 0, axis_index_groups=same_core, tiled=True
+        )
+        piece = jnp.take(got, owners // cores, axis=0, mode="clip")
+        low, high = piece[:, :half], piece[:, half:]
+        theirs = lax.ppermute(jnp.where(core == 0, high, low), "rows", swap)
+        ours = jnp.where(core == 0, low, high)
+        piece = jnp.where((owners % cores == core)[:, None, None], ours, theirs)
         here = lax.all_gather(piece, "rows", axis_index_groups=same_core)
         there = lax.ppermute(here, "rows", swap)
         inno, y, cross_x, cross_h = cross_products(which, here, there, state, predicted)

time: 283 us -> 284 us (level)
  waiting for transfers between devices: 103 us -> 99.1 us
  blocking collectives: 58.3 us -> 62 us
    all_to_all x1, waiting for transfers between devices: 33.7 us -> 29 us  [on_device(): lax.all_to_all(out.reshape(n_z, cores * half, local), 'rows', 0, 0, axis_...]
    all_gather x1, blocking collectives: 30.6 us -> 34.9 us  [on_device(): here = lax.all_gather(piece, 'rows', axis_index_groups=same_core)]
  transfers between devices with their start and end apart: 5 -> 6, of which waited for: 5 -> 6; matrix products, arithmetic and copies ran while one was open for 1% -> 1% of each run, Pallas kernels for 19% -> 19%
where the time goes in v3:
time: 284 us; the launch traced here: 283 us
  waiting for transfers between devices  99.1 us (35%)
  Pallas kernels  74.9 us (26%)
  blocking collectives  62 us (22%)
  starting transfers between devices  28.6 us (10%)
  between operations  14.2 us (5%)
  local copies, waits for them, and re-layouts  3.52 us (1%)
    pallas_call x1, Pallas kernels, chain(): pl.pallas_call(functools.partial(chain_kernel, local, scale), out_shape=j...  49.4 us
    all_gather x1, blocking collectives, on_device(): here = lax.all_gather(piece, 'rows', axis_index_groups=same_core)  34.9 us
    psum x1, waiting for transfers between devices, on_device(): cross_x, cross_h = lax.psum((cross_x, cross_h), 'mem')  32.7 us
    all_to_all x1, waiting for transfers between devices, on_device(): got = lax.all_to_all(payload, 'mem', 0, 0, tiled=True)  31.7 us
    all_to_all x1, waiting for transfers between devices, on_device(): lax.all_to_all(out.reshape(n_z, cores * half, local), 'rows', 0, 0, axis_...  29 us
    all_to_all x1, blocking collectives, on_device(): lax.all_to_all(jnp.broadcast_to(summed[None], (n_mem, n_gram, p)), 'mem',...  27.1 us
    all_to_all x1, starting transfers between devices, on_device(): lax.all_to_all(out.reshape(n_z, cores * half, local), 'rows', 0, 0, axis_...  15.2 us
    all_to_all x1, starting transfers between devices, on_device(): got = lax.all_to_all(payload, 'mem', 0, 0, tiled=True)  7.42 us
  transfers between devices with their start and end apart: 6, of which 6 were waited for; matrix products, arithmetic and copies ran while one was open for 1% of the time, Pallas kernels for 19%

profile of v3, /device:TPU:6, one launch (start us, length us, event | category | flops | bytes accessed | tf_op | source)
XLA Modules:
  0.0 283.2 jit_solution(3914067881020945095)
XLA Ops:
  7.2 0.0 copy-start.4
  7.2 3.1 %pick.1 = f32[32,16,256]{2,1,0:T(8,128)} custom-call(s32[1]{0:T(128)} %bitcast.1.row_ref, s32[3]{0:T(128)} %owners_ref.1, s32[3,256]{1,0:T(4,128)} %positions_ref.1, f32[384,256]{1,0:T(8,128)} %pred_ref.7, f32[384,256]{1,0:T(8,128)} %pert_ref.1), custom_call_target="tpu_custom_call" | custom-call | tf_op jit(solution)/shard_map/pick/pallas_call | solution.py:232
  10.3 15.2 %all-to-all-start = ((f32[16,32,256]{2,1,0:T(8,128)}), f32[16,32,256]{2,1,0:T(8,128)S(1)}, u32[]{:S(2)}, u32[]{:S(2)}) async-start(f32[16,32,256]{2,1,0:T(8,128)} %bitcast.11), calls=%async_computation | async-start | bytes 1048576 | tf_op jit(solution)/shard_map/all_to_all | solution.py:427
  25.5 0.0 copy-done.4
  25.6 29.0 %all-to-all-done = f32[16,32,256]{2,1,0:T(8,128)S(1)} async-done(((f32[16,32,256]{2,1,0:T(8,128)}), f32[16,32,256]{2,1,0:T(8,128)S(1)}, u32[]{:S(2)}, u32[]{:S(2)}) %all-to-all-start) | async-done | bytes 524320 | tf_op jit(solution)/shard_map/all_to_all | solution.py:427
  54.6 0.6 gather_fusion
  55.2 1.9 collective-permute-start
  57.1 1.2 collective-permute-done
  58.3 0.1 select_select_fusion
  58.4 34.9 %all-gather = f32[48,16,256]{2,1,0:T(8,128)S(1)} all-gather(f32[3,16,256]{2,1,0:T(8,128)S(1)} %select_select_fusion), channel_id=2, replica_groups={{0,32,64,96,128,160,192,224,256,288,320,352,384,416,448,480},{16,48,80,..., dimensions={0}, use_global_device_ids=true | all-gather | bytes 835584 | tf_op jit(solution)/shard_map/all_gather | solution.py:435
  93.3 1.9 collective-permute-start.1
  95.2 2.3 collective-permute-done.1.there_ref
  97.5 0.9 copy-done.3
  98.3 7.2 %cross.1 = (f32[768,256]{1,0:T(8,128)}, f32[1280,256]{1,0:T(8,128)}, f32[512,1280]{1,0:T(8,128)}, f32[384,1280]{1,0:T(8,128)}) custom-call(s32[1]{0:T(128)} %bitcast.core_ref, f32[16,3,16,256]{3,2,1,0:T(8,128)} %bitcast.10, f32[16,3,16,256]{3,2,1,0:T(8,128)} %copy-done.3, f32[512,256]{1,0:T(8,128)} %state_ref.5, f32[384,256]{1,0:T(8,128)} %pred_ref.7), custom_call_target="tpu_custom_call" | custom-call | tf_op jit(solution)/shard_map/cross/pallas_call | solution.py:286
  105.6 5.5 %gram.1 = f32[16,112,256]{2,1,0:T(8,128)} custom-call(s32[1]{0:T(128)} %bitcast.core_ref, f32[1280,256]{1,0:T(8,128)} %get-tuple-element.9.raw_ref, f32[512,256]{1,0:T(8,128)} %state_ref.5, f32[384,256]{1,0:T(8,128)} %pred_ref.7), custom_call_target="tpu_custom_call" | custom-call | tf_op jit(solution)/shard_map/gram/pallas_call | solution.py:335
  111.0 7.4 %all-to-all-start.1 = ((f32[16,112,256]{2,1,0:T(8,128)}), f32[16,112,256]{2,1,0:T(8,128)S(1)}, u32[]{:S(2)}, u32[]{:S(2)}) async-start(f32[16,112,256]{2,1,0:T(8,128)} %gram.1), calls=%async_computation.1 | async-start | bytes 3670016 | tf_op jit(solution)/shard_map/all_to_all | solution.py:441
  118.4 0.0 all-reduce.3.cloned.1.call-start
  118.5 0.7 all-reduce.3.cloned.1.call-update
  119.2 31.7 %all-to-all-done.1 = f32[16,112,256]{2,1,0:T(8,128)S(1)} async-done(((f32[16,112,256]{2,1,0:T(8,128)}), f32[16,112,256]{2,1,0:T(8,128)S(1)}, u32[]{:S(2)}, u32[]{:S(2)}) %all-to-all-start.1) | async-done | bytes 1835040 | tf_op jit(solution)/shard_map/all_to_all | solution.py:441
  150.8 0.1 slice_reduce_fusion
  150.9 0.1 broadcast_in_dim.22
  151.1 27.1 %all_to_all.15 = f32[16,96,256]{2,1,0:T(8,128)S(1)} all-to-all(f32[16,96,256]{2,1,0:T(8,128)S(1)} %broadcast_in_dim.22), channel_id=1, replica_groups=mesh['rows'=32,'mem'=16] {'mem'}, dimensions={0} | all-to-all | bytes 3145728 | tf_op jit(solution)/shard_map/all_to_all | solution.py:449
  178.2 2.1 collective-permute-start.2
  180.3 0.2 copy.8
  180.5 0.6 concatenate.4.sums_ref
  181.1 0.6 slice_subtract_fusion.dev_ref
  181.8 1.7 collective-permute-done.2.there_ref
  183.5 1.1 copy-done.2
  184.6 49.4 %chain.1.v_ref = f32[1280,256]{1,0:T(8,128)} custom-call(s32[1]{0:T(128)} %bitcast.core_ref, f32[1536,256]{1,0:T(8,128)} %bitcast.8, f32[1536,256]{1,0:T(8,128)} %copy-done.2, f32[16,1280]{1,0:T(8,128)} %slice_subtract_fusion.dev_ref, f32[3,256]{1,0:T(4,128)} %r_ref.1, f32[768,256]{1,0:T(8,128)} %get-tuple-element.10.e_ref), custom_call_target="tpu_custom_call" | custom-call | tf_op jit(solution)/shard_map/chain/pallas_call | solution.py:189
  234.0 4.1 %base.1 = (f32[512,256]{1,0:T(8,128)}, f32[384,256]{1,0:T(8,128)}, bf16[3840,256]{1,0:T(8,128)(2,1)}) custom-call(f32[512,256]{1,0:T(8,128)} %state_ref.5, f32[384,256]{1,0:T(8,128)} %pred_ref.7, f32[16,896]{1,0:T(8,128)} %concatenate.4.sums_ref, f32[16,1280]{1,0:T(8,128)} %slice_subtract_fusion.dev_ref, f32[1280,256]{1,0:T(8,128)} %chain.1.v_ref), custom_call_target="tpu_custom_call" | custom-call | tf_op jit(solution)/shard_map/base/pallas_call | solution.py:374
  238.1 32.7 %all-reduce.3.cloned.1.call-done = (f32[512,1280]{1,0:T(8,128)}, f32[384,1280]{1,0:T(8,128)}) async-done(((f32[512,1280]{1,0:T(8,128)}, f32[384,1280]{1,0:T(8,128)}), (f32[512,1280]{1,0:T(8,128)}, f32[384,1280]{1,0:T(8,128)})) %all-reduce.3.cloned.1.call-update) | async-done | bytes 4587536 | tf_op jit(solution)/shard_map/psum | solution.py:439
  270.7 5.6 %update.1 = (f32[512,256]{1,0:T(8,128)}, f32[384,256]{1,0:T(8,128)}) custom-call(f32[512,256]{1,0:T(8,128)} %get-tuple-element.11.base_x_ref, f32[384,256]{1,0:T(8,128)} %get-tuple-element.12.base_h_ref, f32[512,1280]{1,0:T(8,128)} %get-tuple-element.16.cross_x_ref, f32[384,1280]{1,0:T(8,128)} %get-tuple-element.17.cross_h_ref, ...), custom_call_target="tpu_custom_call" | custom-call | tf_op jit(solution)/shard_map/update/pallas_call | solution.py:392
  (13 shorter events, 0.1 us)
Async XLA Ops:
  7.2 18.4 %copy-start.4 = (s32[3]{0:T(128)S(1)}, s32[3]{0:T(128)}, u32[]{:S(2)}) copy-start(s32[3]{0:T(128)} %owners_ref.1) | copy-start | bytes 40
  10.3 44.3 %all-to-all-start = ((f32[16,32,256]{2,1,0:T(8,128)}), f32[16,32,256]{2,1,0:T(8,128)S(1)}, u32[]{:S(2)}, u32[]{:S(2)}) async-start(f32[16,32,256]{2,1,0:T(8,128)} %bitcast.11), calls=%async_computation | async-start | bytes 1048576 | tf_op jit(solution)/shard_map/all_to_all | solution.py:427
  55.2 3.1 %collective-permute-start = (f32[3,16,256]{2,1,0:T(8,128)S(1)}, f32[3,16,256]{2,1,0:T(8,128)S(1)}, u32[]{:S(2)}, u32[]{:S(2)}) collective-permute-start(f32[3,16,256]{2,1,0:T(8,128)S(1)} %slice_select_fusion), channel_id=1, source_target_pairs={{0,16},{16,0},{32,48},{48,32},{64,80},{80,64},{96,112},{112,96},{1... | collective-permute-start | bytes 147464 | tf_op jit(solution)/shard_map/ppermute | solution.py:432
  93.3 4.2 %copy-start.1 = (f32[48,16,256]{2,1,0:T(8,128)}, f32[48,16,256]{2,1,0:T(8,128)S(1)}, u32[]{:S(2)}) copy-start(f32[48,16,256]{2,1,0:T(8,128)S(1)} %all-gather) | copy-start | bytes 2359300
  93.3 4.2 %collective-permute-start.1 = (f32[16,3,16,256]{3,2,1,0:T(8,128)S(1)}, f32[16,3,16,256]{3,2,1,0:T(8,128)S(1)}, u32[]{:S(2)}, u32[]{:S(2)}) collective-permute-start(f32[16,3,16,256]{3,2,1,0:T(8,128)S(1)} %bitcast.9), channel_id=1, source_target_pairs={{0,16},{16,0},{32,48},{48,32},{64,80},{80,64},{96,112},{112,96},{1... | collective-permute-start | bytes 2359304 | tf_op jit(solution)/shard_map/ppermute | solution.py:436
  97.4 0.9 copy-start.3
  111.0 39.8 %all-to-all-start.1 = ((f32[16,112,256]{2,1,0:T(8,128)}), f32[16,112,256]{2,1,0:T(8,128)S(1)}, u32[]{:S(2)}, u32[]{:S(2)}) async-start(f32[16,112,256]{2,1,0:T(8,128)} %gram.1), calls=%async_computation.1 | async-start | bytes 3670016 | tf_op jit(solution)/shard_map/all_to_all | solution.py:441
  118.4 152.3 %all-reduce.3.cloned.1.call-start = ((), (), s32[]{:S(2)}) async-start(), calls=%async_computation.3 | async-start | bytes 9175040 | tf_op jit(solution)/shard_map/psum | solution.py:439
  178.2 6.4 %copy-start = (f32[16,96,256]{2,1,0:T(8,128)}, f32[16,96,256]{2,1,0:T(8,128)S(1)}, u32[]{:S(2)}) copy-start(f32[16,96,256]{2,1,0:T(8,128)S(1)} %all_to_all.15) | copy-start | bytes 4718596
  178.2 5.3 %collective-permute-start.2 = (f32[1536,256]{1,0:T(8,128)S(1)}, f32[1536,256]{1,0:T(8,128)S(1)}, u32[]{:S(2)}, u32[]{:S(2)}) collective-permute-start(f32[1536,256]{1,0:T(8,128)S(1)} %bitcast.7), channel_id=1, source_target_pairs={{0,16},{16,0},{32,48},{48,32},{64,80},{80,64},{96,112},{112,96},{1... | collective-permute-start | bytes 4718600 | tf_op jit(solution)/shard_map/ppermute | solution.py:452
  183.5 1.1 copy-start.2
Sparse Core Ops, SparseCore 0:
  122.7 147.9 all-reduce.2
